TPU v7x, 32 devices: a whole 2x2x4 slice. The times are simulated.
32 devices in a mesh: ctx: 2 (over core), shard: 16 (over z, y, x).
Axes of the slice: x: 2, y: 2, z: 4, core: 2. Of those that a mesh axis runs over, the one named last changes fastest.
Arguments:
- tokens: bfloat16 [2, 16, 1024, 768], P(None, 'shard', 'ctx'), may hold values from -6 to 6
- cotangent: bfloat16 [2, 16, 1024, 768], P(None, 'shard', 'ctx'), may hold values from -6 to 6
- segment_ids: int32 [2, 16, 1024], P(None, 'shard', 'ctx'), may hold values from 0 to 1, never falling along the last dimension, each value on 1 to 896 neighbouring positions
- padding: int32 [2, 16, 1024], P(None, 'shard', 'ctx'), may hold values 0 or 1
- routes: int32 [2, 16, 1024, 1], P(None, 'shard', 'ctx'), may hold values from 0 to 15; in each aligned block of 512 rows (0 to 511, 512 to 1023, ..., all dimensions but the last counted through in order) at most 64 rows name the same one
- norm_one_gain: bfloat16 [768], replicated, may hold values from 0.5 to 1.5
- qkv_weight: bfloat16 [768, 2304], P('shard'), may hold values from -0.21875 to 0.21875
- out_weight: bfloat16 [768, 768], P('shard'), may hold values from -1.75 to 1.75
- norm_two_gain: bfloat16 [768], replicated, may hold values from 0.5 to 1.5
- centroids: bfloat16 [768, 16], replicated, may hold values from -0.15625 to 0.15625
- expert_in: bfloat16 [16, 768, 3072], P('shard'), may hold values from -0.21875 to 0.21875
- expert_out: bfloat16 [16, 3072, 768], P('shard'), may hold values from -0.21875 to 0.21875
Outputs:
- block_out: bfloat16 [2, 16, 1024, 768], P(None, 'shard', 'ctx')
- grad_tokens: float32 [2, 16, 1024, 768], P(None, 'shard', 'ctx')
- grad_norm_one: float32 [768], P(('ctx', 'shard'))
- grad_qkv: float32 [768, 2304], P(('ctx', 'shard'))
- grad_out_proj: float32 [768, 768], P(('ctx', 'shard'))
- grad_norm_two: float32 [768], P(('ctx', 'shard'))
- grad_centroids: float32 [768, 16], P(('ctx', 'shard'))
- grad_expert_in: float32 [16, 768, 3072], P('shard', None, 'ctx')
- grad_expert_out: float32 [16, 3072, 768], P('shard', 'ctx')
Inputs may be any that keep to these rules, and one draw needn't show every extreme that they name: `segment_ids`: segment ids never fall along a sequence; each sequence holds two documents, each of at least 128 and at most 896 positions; where the split falls varies from sequence to sequence. `routes`: within each aligned block of 512 positions of a sequence, no expert is named more than 64 times; some block names some expert exactly 64 times.
All inputs are finite; a program needn't handle non-finite values. No bound on the sum of `padding` on one device may be relied on, other than what follows from the above.
Results may differ from a plain program's by a relative error of at most 0.013.
Values may be sent and summed in bfloat16 or wider, within the bound.
A program may use at most 384 MiB of HBM per device.

v0:
```python
import jax
import jax.numpy as jnp
from jax import lax
from jax.sharding import PartitionSpec as P

D = 768
HEADS = 12
HEAD_DIM = 64
FF = 3072
MICRO = 2


EPSILON = 1e-05
NEGATIVE = -1e30
HIGH = lax.Precision.HIGHEST


def layer_norm(values, gain_vec):
    centre = values - jnp.mean(values, axis=1, keepdims=True)
    spread = jnp.mean(centre * centre, axis=1, keepdims=True)
    return centre * lax.rsqrt(spread + EPSILON) * gain_vec


def gelu_tanh(values):
    return jax.nn.gelu(values, approximate=True)


def masked_scores(queries, key_heads, query_pos, key_pos, query_doc, key_doc, key_pad):
    scores = jnp.einsum(
        "qhd,khd->hqk", queries, key_heads, preferred_element_type=jnp.float32
    ) * HEAD_DIM ** (-0.5)
    allowed = (query_doc[:, None] == key_doc[None, :]) & (key_pos[None, :] <= query_pos[:, None])
    allowed = allowed & ((key_pad[None, :] == 1) | (key_pos[None, :] == query_pos[:, None]))
    return jnp.where(allowed[None], scores, NEGATIVE)


def rows_first(left, right):
    return lax.dot_general(
        left, right, (((0,), (0,)), ((), ())), preferred_element_type=jnp.float32
    )


def rows_last(left, right):
    return lax.dot_general(
        left, right, (((1,), (1,)), ((), ())), preferred_element_type=jnp.float32
    )


def body(
    tokens,
    cotangent,
    segment_ids,
    padding,
    routes,
    norm_one_gain,
    qkv_weight,
    out_weight,
    norm_two_gain,
    centroids,
    expert_in,
    expert_out,
):
    local_len = tokens.shape[2]
    experts = centroids.shape[1]
    capacity = max(2, 2 * local_len // experts)
    seq_len = local_len * lax.axis_size("ctx")
    qkv_full, out_full = (
        lax.all_gather(qkv_weight, "shard", axis=0, tiled=True),
        lax.all_gather(out_weight, "shard", axis=0, tiled=True),
    )
    gain_one = norm_one_gain.astype(jnp.float32)
    gain_two = norm_two_gain.astype(jnp.float32)
    centre_f = centroids.astype(jnp.float32)
    up_local = expert_in[0]
    down_local = expert_out[0]
    query_pos = lax.axis_index("ctx") * local_len + jnp.arange(local_len, dtype=jnp.int32)
    all_pos = jnp.arange(seq_len, dtype=jnp.int32)
    slot_ids = jnp.arange(experts * capacity, dtype=jnp.int32)
    expert_ids = jnp.arange(experts, dtype=jnp.int32)
    score_scale = HEAD_DIM ** (-0.5)
    grad_qkv_sum = jnp.zeros((D, 3 * D), jnp.float32)
    grad_out_sum = jnp.zeros((D, D), jnp.float32)
    grad_one_sum = jnp.zeros((D,), jnp.float32)
    grad_two_sum = jnp.zeros((D,), jnp.float32)
    grad_centre = jnp.zeros((D, experts), jnp.float32)
    grad_up_sum = jnp.zeros((D, FF), jnp.float32)
    grad_down_sum = jnp.zeros((D, FF), jnp.float32)
    block_list = []
    input_list = []
    for micro_index in range(MICRO):
        inputs = tokens[micro_index, 0].astype(jnp.float32)
        doc_ids = segment_ids[micro_index, 0]
        pad_mask = padding[micro_index, 0]
        route_ids = routes[micro_index, 0, :, 0]
        normed_one, norm_one_back = jax.vjp(layer_norm, inputs, gain_one)
        first_bf = normed_one.astype(jnp.bfloat16)
        qkv = jnp.dot(first_bf, qkv_full, preferred_element_type=jnp.float32)
        queries = qkv[:, :D].astype(jnp.bfloat16)
        key_rows = qkv[:, D : 2 * D].astype(jnp.bfloat16)
        value_rows = qkv[:, 2 * D :].astype(jnp.bfloat16)
        key_all, value_all, doc_all, pad_all = (
            lax.all_gather(key_rows, "ctx", axis=0, tiled=True),
            lax.all_gather(value_rows, "ctx", axis=0, tiled=True),
            lax.all_gather(doc_ids, "ctx", axis=0, tiled=True),
            lax.all_gather(pad_mask, "ctx", axis=0, tiled=True),
        )
        query_heads = queries.reshape(local_len, HEADS, HEAD_DIM)
        key_heads = key_all.reshape(seq_len, HEADS, HEAD_DIM)
        value_heads = value_all.reshape(seq_len, HEADS, HEAD_DIM)
        scores = masked_scores(
            query_heads, key_heads, query_pos, all_pos, doc_ids, doc_all, pad_all
        )
        row_max = jnp.max(scores, axis=2, keepdims=True)
        weights = jnp.exp(scores - row_max)
        row_total = jnp.sum(weights, axis=2, keepdims=True)
        probs_now = weights / row_total
        log_total = row_max + jnp.log(row_total)
        attended = jnp.einsum(
            "hqk,khd->qhd",
            probs_now.astype(jnp.bfloat16),
            value_heads,
            preferred_element_type=jnp.float32,
        )
        attended = attended.reshape(local_len, D).astype(jnp.bfloat16)
        residual = inputs + jnp.dot(attended, out_full, preferred_element_type=jnp.float32)
        normed_two, norm_two_back = jax.vjp(layer_norm, residual, gain_two)
        second_bf = normed_two.astype(jnp.bfloat16)
        choose_mask = route_ids[:, None] == expert_ids[None, :]
        choose_f = choose_mask.astype(jnp.float32)
        logit = jnp.sum(
            jnp.dot(second_bf, centroids, preferred_element_type=jnp.float32) * choose_f, axis=1
        )
        gate_value = jax.nn.sigmoid(logit)
        choose_int = choose_mask.astype(jnp.int32)
        counts = jnp.cumsum(choose_int, axis=0)
        slot_rank = jnp.sum(counts * choose_int, axis=1) - 1
        target = route_ids * capacity + slot_rank
        dispatch = (slot_ids[:, None] == target[None, :]).astype(jnp.bfloat16)
        outbound = jnp.dot(dispatch, second_bf, preferred_element_type=jnp.float32).astype(
            jnp.bfloat16
        )
        outbound = outbound.reshape(experts, capacity, D)
        received = lax.all_to_all(outbound, "shard", split_axis=0, concat_axis=0, tiled=True)
        slot_rows = received.reshape(-1, D)
        upward = jnp.dot(slot_rows, up_local, preferred_element_type=jnp.float32)
        hidden = gelu_tanh(upward).astype(jnp.bfloat16)
        result = jnp.dot(hidden, down_local, preferred_element_type=jnp.float32).astype(
            jnp.bfloat16
        )
        returned = lax.all_to_all(
            result.reshape(received.shape), "shard", split_axis=0, concat_axis=0, tiled=True
        )
        returned, received, upward = (
            returned,
            received,
            upward.reshape(received.shape[0], received.shape[1], FF),
        )
        expert_rows = rows_first(dispatch, returned.reshape(experts * capacity, D))
        block_list.append((residual + gate_value[:, None] * expert_rows).astype(jnp.bfloat16))
        grad_out = cotangent[micro_index, 0].astype(jnp.float32)
        grad_gate = jnp.sum(grad_out * expert_rows, axis=1)
        grad_logit = grad_gate * gate_value * (1.0 - gate_value)
        grad_rows = (gate_value[:, None] * grad_out).astype(jnp.bfloat16)
        grad_outbound = jnp.dot(dispatch, grad_rows, preferred_element_type=jnp.float32).astype(
            jnp.bfloat16
        )
        grad_received = lax.all_to_all(
            grad_outbound.reshape(experts, capacity, D),
            "shard",
            split_axis=0,
            concat_axis=0,
            tiled=True,
        )
        grad_result = grad_received.reshape(-1, D)
        hidden_again, gelu_back = jax.vjp(gelu_tanh, upward.reshape(-1, FF))
        grad_down_sum = grad_down_sum + rows_first(grad_result, hidden_again.astype(jnp.bfloat16))
        grad_hidden = rows_last(grad_result, down_local)
        grad_upward = gelu_back(grad_hidden)[0].astype(jnp.bfloat16)
        grad_up_sum = grad_up_sum + rows_first(received.reshape(-1, D), grad_upward)
        grad_send = (
            rows_last(grad_upward, up_local).astype(jnp.bfloat16).reshape(grad_received.shape)
        )
        grad_back = lax.all_to_all(grad_send, "shard", split_axis=0, concat_axis=0, tiled=True)
        grad_second = rows_first(dispatch, grad_back.reshape(experts * capacity, D))
        grad_second = grad_second + grad_logit[:, None] * jnp.dot(
            choose_f, centre_f.T, precision=HIGH
        )
        grad_centre = grad_centre + jnp.dot(
            second_bf.astype(jnp.float32).T, choose_f * grad_logit[:, None], precision=HIGH
        )
        grad_resid_norm, grad_two_term = norm_two_back(grad_second)
        grad_residual = grad_out + grad_resid_norm
        grad_two_sum = grad_two_sum + grad_two_term
        grad_branch = grad_residual.astype(jnp.bfloat16)
        grad_out_sum = grad_out_sum + rows_first(attended, grad_branch)
        grad_attend = (
            rows_last(grad_branch, out_full)
            .astype(jnp.bfloat16)
            .reshape(local_len, HEADS, HEAD_DIM)
        )
        probs_again = jnp.exp(
            masked_scores(query_heads, key_heads, query_pos, all_pos, doc_ids, doc_all, pad_all)
            - log_total
        )
        grad_probs = jnp.einsum(
            "qhd,khd->hqk", grad_attend, value_heads, preferred_element_type=jnp.float32
        )
        row_terms = jnp.sum(probs_again * grad_probs, axis=2, keepdims=True)
        grad_scores = (probs_again * (grad_probs - row_terms)).astype(jnp.bfloat16)
        grad_query = (
            jnp.einsum("hqk,khd->qhd", grad_scores, key_heads, preferred_element_type=jnp.float32)
            * score_scale
        )
        grad_key_all = (
            jnp.einsum("hqk,qhd->khd", grad_scores, query_heads, preferred_element_type=jnp.float32)
            * score_scale
        )
        grad_value_all = jnp.einsum(
            "hqk,qhd->khd",
            probs_again.astype(jnp.bfloat16),
            grad_attend,
            preferred_element_type=jnp.float32,
        )
        grad_key, grad_value = (
            lax.psum_scatter(
                grad_key_all.reshape(seq_len, D).astype(jnp.bfloat16),
                "ctx",
                scatter_dimension=0,
                tiled=True,
            ).astype(jnp.float32),
            lax.psum_scatter(
                grad_value_all.reshape(seq_len, D).astype(jnp.bfloat16),
                "ctx",
                scatter_dimension=0,
                tiled=True,
            ).astype(jnp.float32),
        )
        grad_qkv_rows = jnp.concatenate(
            [grad_query.reshape(local_len, D), grad_key, grad_value], axis=1
        ).astype(jnp.bfloat16)
        grad_qkv_sum = grad_qkv_sum + rows_first(first_bf, grad_qkv_rows)
        grad_first = rows_last(grad_qkv_rows, qkv_full)
        grad_in_norm, grad_one_term = norm_one_back(grad_first)
        grad_one_sum = grad_one_sum + grad_one_term
        input_list.append(grad_residual + grad_in_norm)
    dense_sums = (
        lax.psum_scatter(grad_one_sum, ("ctx", "shard"), scatter_dimension=0, tiled=True),
        lax.psum_scatter(grad_qkv_sum, ("ctx", "shard"), scatter_dimension=0, tiled=True),
        lax.psum_scatter(grad_out_sum, ("ctx", "shard"), scatter_dimension=0, tiled=True),
        lax.psum_scatter(grad_two_sum, ("ctx", "shard"), scatter_dimension=0, tiled=True),
        lax.psum_scatter(grad_centre, ("ctx", "shard"), scatter_dimension=0, tiled=True),
    )
    expert_sums = (
        lax.psum_scatter(
            grad_up_sum.astype(jnp.bfloat16), "ctx", scatter_dimension=1, tiled=True
        ).astype(jnp.float32),
        lax.psum_scatter(
            grad_down_sum.astype(jnp.bfloat16), "ctx", scatter_dimension=1, tiled=True
        ).astype(jnp.float32),
    )
    block_out = jnp.stack(block_list)[:, None]
    grad_tokens = jnp.stack(input_list)[:, None]
    return (
        block_out,
        grad_tokens,
        dense_sums[0],
        dense_sums[1],
        dense_sums[2],
        dense_sums[3],
        dense_sums[4],
        expert_sums[0][None],
        expert_sums[1].T[None],
    )


def solution(mesh):
    in_specs = (
        P(None, "shard", "ctx", None),
        P(None, "shard", "ctx", None),
        P(None, "shard", "ctx"),
        P(None, "shard", "ctx"),
        P(None, "shard", "ctx", None),
        P(),
        P("shard", None),
        P("shard", None),
        P(),
        P(),
        P("shard", None, None),
        P("shard", None, None),
    )
    out_specs = (
        P(None, "shard", "ctx", None),
        P(None, "shard", "ctx", None),
        P(("ctx", "shard")),
        P(("ctx", "shard"), None),
        P(("ctx", "shard"), None),
        P(("ctx", "shard")),
        P(("ctx", "shard"), None),
        P("shard", None, "ctx"),
        P("shard", "ctx", None),
    )
    return jax.shard_map(body, mesh=mesh, in_specs=in_specs, out_specs=out_specs, check_vma=False)
```

profile of v0, /device:TPU:0, one launch (start us, length us, event | category | flops | bytes accessed | tf_op | source)
XLA Modules:
  0.0 985.1 jit_solution(11996730696689875057)
XLA Ops:
  11.0 73.8 %all-gather.11.cloned.1.call-done = bf16[768,2304]{1,0:T(8,128)(2,1)} async-done(((bf16[48,2304]{1,0:T(8,128)(2,1)}), bf16[768,2304]{1,0:T(8,128)(2,1)}) %all-gather.11.cloned.1.call-update) | async-done | bytes 3538960 | tf_op jit(solution)/shard_map/all_gather | solution.py:68
  112.8 12.7 %fusion.27 = (f32[12,512]{1,0:T(8,128)S(1)}, f32[12,512,1024]{2,1,0:T(8,128)}) fusion(pred[512,1024]{1,0:T(8,128)(4,1)} %get-tuple-element.91, bf16[512,12,64]{0,2,1:T(8,128)(2,1)} %bitcast.293, bf16[1024,12,64]{0,2,1:T(8,128)(2,1)S(1)} %bitcast.289), kind=kOutput, calls=%fused_computation.45 | convolution fusion | flops 824174592 | bytes 28073984 | tf_op jit(solution)/shard_map/qhd,khd->hqk/dot_general | solution.py:29
  125.5 11.8 %fusion.1 = f32[12,512]{1,0:T(8,128)S(1)} fusion(f32[12,512]{1,0:T(8,128)S(1)} %get-tuple-element.96, f32[12,512,1024]{2,1,0:T(8,128)} %get-tuple-element.97, pred[512,1024]{1,0:T(8,128)(4,1)S(1)} %copy-done.14), kind=kLoop, calls=%fused_computation.13 | loop fusion | flops 25159680 | bytes 25739264 | tf_op jit(solution)/shard_map/reduce_sum | solution.py:115
  140.0 12.7 %fusion.112 = bf16[12,64,512]{2,1,0:T(8,128)(2,1)} fusion(bf16[1024,12,64]{0,2,1:T(8,128)(2,1)} %bitcast.299, f32[12,512]{1,0:T(8,128)S(1)} %fusion.1, f32[12,512]{1,0:T(8,128)S(1)} %get-tuple-element.96, f32[12,512,1024]{2,1,0:T(8,128)} %get-tuple-element.97, pred[512,1024]{1,0:T(8,128)(4,1)S(1)} %copy-done.15), kind=kOutput, calls=%fused_computation.162 | convolution fusion | flops 837156864 | bytes 28098560 | tf_op jit(solution)/shard_map/hqk,khd->qhd/dot_general | solution.py:118
  152.7 19.3 %all-gather.17.cloned.1.call-done = bf16[768,768]{1,0:T(8,128)(2,1)} async-done(((bf16[48,768]{1,0:T(8,128)(2,1)}), bf16[768,768]{1,0:T(8,128)(2,1)}) %all-gather.17.cloned.1.call-update) | async-done | bytes 1179664 | tf_op jit(solution)/shard_map/all_gather | solution.py:69
  174.7 7.9 all-gather.15.cloned.1.call-done
  185.6 15.0 %fusion.26 = (f32[12,512]{1,0:T(8,128)S(1)}, f32[12,512,1024]{2,1,0:T(8,128)}) fusion(pred[512,1024]{1,0:T(8,128)(4,1)} %get-tuple-element.90, bf16[512,12,64]{0,2,1:T(8,128)(2,1)} %bitcast.295, bf16[1024,12,64]{0,2,1:T(8,128)(2,1)} %bitcast.291), kind=kOutput, calls=%fused_computation.44 | convolution fusion | flops 824174592 | bytes 28073984 | tf_op jit(solution)/shard_map/qhd,khd->hqk/dot_general | solution.py:29
  200.6 11.8 %fusion = f32[12,512]{1,0:T(8,128)S(1)} fusion(f32[12,512]{1,0:T(8,128)S(1)} %get-tuple-element.92, f32[12,512,1024]{2,1,0:T(8,128)} %get-tuple-element.93, pred[512,1024]{1,0:T(8,128)(4,1)S(1)} %copy-done.17), kind=kLoop, calls=%fused_computation.12 | loop fusion | flops 25159680 | bytes 25739264 | tf_op jit(solution)/shard_map/reduce_sum | solution.py:115
  215.0 11.9 %fusion.113 = bf16[12,64,512]{2,1,0:T(8,128)(2,1)S(1)} fusion(bf16[1024,12,64]{0,2,1:T(8,128)(2,1)} %bitcast.301, f32[12,512]{1,0:T(8,128)S(1)} %fusion, f32[12,512]{1,0:T(8,128)S(1)} %get-tuple-element.92, f32[12,512,1024]{2,1,0:T(8,128)} %get-tuple-element.93, pred[512,1024]{1,0:T(8,128)(4,1)} %get-tuple-element.90), kind=kOutput, calls=%fused_computation.163 | convolution fusion | flops 837156864 | bytes 28098560 | tf_op jit(solution)/shard_map/hqk,khd->qhd/dot_general | solution.py:118
  241.8 30.6 %all-to-all-done.2 = bf16[16,64,768]{2,1,0:T(8,128)(2,1)} async-done(((bf16[16,64,768]{2,1,0:T(8,128)(2,1)}), bf16[16,64,768]{2,1,0:T(8,128)(2,1)}, u32[]{:S(2)}, u32[]{:S(2)}) %all-to-all-start.2) | async-done | bytes 1572896 | tf_op jit(solution)/shard_map/all_to_all | solution.py:143
  272.3 8.3 all-to-all-start
  280.7 7.4 fusion.40
  292.6 10.7 %fusion.91 = bf16[1024,768]{1,0:T(8,128)(2,1)} fusion(bf16[1,3072,768]{2,1,0:T(8,128)(2,1)} %param.23, f32[1024,3072]{1,0:T(8,128)S(1)} %fusion.40), kind=kOutput, calls=%fused_computation.128 | convolution fusion | flops 4860936192 | bytes 18874368 | tf_op jit(solution)/shard_map/dot_general | solution.py:147
  303.2 11.2 %all-to-all-done = bf16[16,64,768]{2,1,0:T(8,128)(2,1)} async-done(((bf16[16,64,768]{2,1,0:T(8,128)(2,1)}), bf16[16,64,768]{2,1,0:T(8,128)(2,1)}, u32[]{:S(2)}, u32[]{:S(2)}) %all-to-all-start) | async-done | bytes 1572896 | tf_op jit(solution)/shard_map/all_to_all | solution.py:143
  314.4 7.3 all-to-all-start.3
  321.8 7.4 fusion.42
  333.7 10.7 %fusion.88 = bf16[1024,768]{1,0:T(8,128)(2,1)} fusion(bf16[1,3072,768]{2,1,0:T(8,128)(2,1)} %param.23, f32[1024,3072]{1,0:T(8,128)S(1)} %fusion.42), kind=kOutput, calls=%fused_computation.127 | convolution fusion | flops 4860936192 | bytes 18874368 | tf_op jit(solution)/shard_map/dot_general | solution.py:147
  344.4 11.0 %all-to-all-done.3 = bf16[16,64,768]{2,1,0:T(8,128)(2,1)} async-done(((bf16[16,64,768]{2,1,0:T(8,128)(2,1)}), bf16[16,64,768]{2,1,0:T(8,128)(2,1)}, u32[]{:S(2)}, u32[]{:S(2)}) %all-to-all-start.3) | async-done | bytes 1572896 | tf_op jit(solution)/shard_map/all_to_all | solution.py:150
  355.5 7.5 all-to-all-start.1
  367.2 29.4 %all-to-all-done.1 = bf16[16,64,768]{2,1,0:T(8,128)(2,1)} async-done(((bf16[16,64,768]{2,1,0:T(8,128)(2,1)}), bf16[16,64,768]{2,1,0:T(8,128)(2,1)}, u32[]{:S(2)}, u32[]{:S(2)}) %all-to-all-start.1) | async-done | bytes 1572896 | tf_op jit(solution)/shard_map/all_to_all | solution.py:150
  403.7 7.4 all-to-all-start.6
  414.9 29.7 %all-to-all-done.6 = bf16[16,64,768]{2,1,0:T(8,128)(2,1)} async-done(((bf16[16,64,768]{2,1,0:T(8,128)(2,1)}), bf16[16,64,768]{2,1,0:T(8,128)(2,1)}, u32[]{:S(2)}, u32[]{:S(2)}) %all-to-all-start.6) | async-done | bytes 1572896 | tf_op jit(solution)/shard_map/all_to_all | solution.py:167
  444.6 7.5 all-to-all-start.4
  452.1 15.3 %fusion.17 = bf16[1024,3072]{1,0:T(8,128)(2,1)S(1)} fusion(f32[1024,3072]{1,0:T(8,128)} %copy-done.93, bf16[1024,768]{1,0:T(8,128)(2,1)} %bitcast.53, bf16[1,3072,768]{2,1,0:T(8,128)(2,1)} %param.23), kind=kOutput, calls=%fused_computation.33 | convolution fusion | flops 4894752768 | bytes 25165824 | tf_op jit(solution)/shard_map/dot_general | solution.py:44
  470.1 8.5 fusion.85
  478.6 7.0 all-to-all-done.4
  485.6 7.8 all-to-all-start.7
  493.4 14.2 %fusion.10 = bf16[1024,3072]{1,0:T(8,128)(2,1)S(1)} fusion(f32[1024,3072]{1,0:T(8,128)} %copy-done.94, bf16[1024,768]{1,0:T(8,128)(2,1)S(1)} %bitcast.309, bf16[1,3072,768]{2,1,0:T(8,128)(2,1)} %param.23), kind=kOutput, calls=%fused_computation.26 | convolution fusion | flops 4894752768 | bytes 25165824 | tf_op jit(solution)/shard_map/dot_general | solution.py:44
  510.2 8.5 fusion.82
  518.7 8.3 all-to-all-done.7
  527.0 7.4 all-to-all-start.5
  540.5 27.5 %all-to-all-done.5 = bf16[16,64,768]{2,1,0:T(8,128)(2,1)} async-done(((bf16[16,64,768]{2,1,0:T(8,128)(2,1)}), bf16[16,64,768]{2,1,0:T(8,128)(2,1)}, u32[]{:S(2)}, u32[]{:S(2)}) %all-to-all-start.5) | async-done | bytes 1572896 | tf_op jit(solution)/shard_map/all_to_all | solution.py:183
  582.4 17.9 %multiply_reduce_fusion.1 = (f32[12,512]{1,0:T(8,128)S(1)}, f32[12,512,1024]{2,1,0:T(8,128)}) fusion(f32[12,512]{1,0:T(8,128)S(1)} %log_add_fusion.1, f32[12,512,1024]{2,1,0:T(8,128)} %get-tuple-element.93, pred[512,1024]{1,0:T(8,128)(4,1)S(1)} %copy-done.18, bf16[512,12,64]{0,2,1:T(8,128)(2,1)} %bitcast.307, bf16[1024,12,64]{0,2,1:T(8,128)(2,1)S(1)} %bitcast.302), kind=kOutput, calls=%fused_computation.4 | convolution fusion | flops 836757504 | bytes 53264384 | tf_op jit(solution)/shard_map/qhd,khd->hqk/dot_general | solution.py:205
  600.3 16.9 %multiply_convert_fusion.1 = bf16[12,512,1024]{2,1,0:T(8,128)(2,1)S(1)} fusion(f32[12,512,1024]{2,1,0:T(8,128)} %get-tuple-element.103, f32[12,512]{1,0:T(8,128)S(1)} %get-tuple-element.102, f32[12,512]{1,0:T(8,128)S(1)} %log_add_fusion.1, f32[12,512,1024]{2,1,0:T(8,128)} %get-tuple-element.93, pred[512,1024]{1,0:T(8,128)(4,1)S(1)} %copy-done.18), kind=kLoop, calls=%fused_computation.3 | loop fusion | flops 37748736 | bytes 63488000 | tf_op jit(solution)/shard_map/convert_element_type | solution.py:209
  625.6 13.8 %fusion.94 = bf16[12,64,1024]{2,1,0:T(8,128)(2,1)} fusion(bf16[512,12,64]{0,2,1:T(8,128)(2,1)S(1)} %bitcast.308, f32[12,512]{1,0:T(8,128)S(1)} %log_add_fusion.1, f32[12,512,1024]{2,1,0:T(8,128)} %get-tuple-element.93, pred[512,1024]{1,0:T(8,128)(4,1)S(1)} %copy-done.18), kind=kOutput, calls=%fused_computation.129 | convolution fusion | flops 831258624 | bytes 28073984 | tf_op jit(solution)/shard_map/hqk,qhd->khd/dot_general | solution.py:218
  640.8 17.9 %multiply_reduce_fusion = (f32[12,512]{1,0:T(8,128)S(1)}, f32[12,512,1024]{2,1,0:T(8,128)}) fusion(f32[12,512]{1,0:T(8,128)S(1)} %log_add_fusion, f32[12,512,1024]{2,1,0:T(8,128)} %get-tuple-element.97, pred[512,1024]{1,0:T(8,128)(4,1)S(1)} %copy-done.16, bf16[512,12,64]{0,2,1:T(8,128)(2,1)} %bitcast.305, bf16[1024,12,64]{0,2,1:T(8,128)(2,1)S(1)} %bitcast.300), kind=kOutput, calls=%fused_computation.1 | convolution fusion | flops 836757504 | bytes 53264384 | tf_op jit(solution)/shard_map/qhd,khd->hqk/dot_general | solution.py:205
  658.6 16.9 %multiply_convert_fusion = bf16[12,512,1024]{2,1,0:T(8,128)(2,1)S(1)} fusion(f32[12,512,1024]{2,1,0:T(8,128)} %get-tuple-element.105, f32[12,512]{1,0:T(8,128)S(1)} %get-tuple-element.104, f32[12,512]{1,0:T(8,128)S(1)} %log_add_fusion, f32[12,512,1024]{2,1,0:T(8,128)} %get-tuple-element.97, pred[512,1024]{1,0:T(8,128)(4,1)S(1)} %copy-done.16), kind=kLoop, calls=%fused_computation | loop fusion | flops 37748736 | bytes 63488000 | tf_op jit(solution)/shard_map/convert_element_type | solution.py:209
  680.6 13.7 %fusion.97 = bf16[12,64,1024]{2,1,0:T(8,128)(2,1)} fusion(bf16[512,12,64]{0,2,1:T(8,128)(2,1)S(1)} %bitcast.306, f32[12,512]{1,0:T(8,128)S(1)} %log_add_fusion, f32[12,512,1024]{2,1,0:T(8,128)} %get-tuple-element.97, pred[512,1024]{1,0:T(8,128)(4,1)S(1)} %copy-done.16), kind=kOutput, calls=%fused_computation.130 | convolution fusion | flops 831258624 | bytes 28073984 | tf_op jit(solution)/shard_map/hqk,qhd->khd/dot_general | solution.py:218
  694.4 8.8 fusion.182
  703.2 10.9 %add_convert_fusion = bf16[768,3072]{1,0:T(8,128)(2,1)} fusion(f32[768,3072]{1,0:T(8,128)S(1)} %fusion.182, bf16[1024,768]{1,0:T(8,128)(2,1)} %bitcast.53, f32[1024,3072]{1,0:T(8,128)} %copy-done.93), kind=kOutput, calls=%fused_computation.42 | convolution fusion | flops 4864868352 | bytes 28311552 | tf_op jit(solution)/shard_map/dot_general | solution.py:38
  714.2 7.8 fusion.193
  722.0 9.7 add_convert_fusion.1
  737.5 10.2 %multiply_convert_fusion.7 = bf16[12,64,512]{2,1,0:T(8,128)(2,1)} fusion(bf16[1024,12,64]{0,2,1:T(8,128)(2,1)S(1)} %bitcast.292, bf16[12,512,1024]{2,1,0:T(8,128)(2,1)} %copy-done.2), kind=kOutput, calls=%fused_computation.151 | convolution fusion | flops 806092800 | bytes 14942208 | tf_op jit(solution)/shard_map/hqk,khd->qhd/dot_general | solution.py:211
  747.7 9.5 multiply_convert_fusion.6
  757.3 6.9 fusion.127
  764.2 8.8 convolution_add_fusion
  786.7 45.5 %all-reduce.3 = (f32[768]{0:T(1024)S(1)}, f32[768]{0:T(1024)S(1)}, f32[768,16]{0,1:T(8,128)S(1)}) all-reduce(f32[768]{0:T(1024)S(1)} %add.227, f32[768]{0:T(1024)S(1)} %add.230, f32[768,16]{0,1:T(8,128)S(1)} %convolution_add_fusion.2), channel_id=10, replica_groups=mesh['ctx'=2,'shard'=16] {'ctx','shard'}, use_global_device_ids=true, to_apply=%region_38.39.clone | all-reduce | flops 13824 | bytes 110592
  854.6 123.7 %reduce-scatter.18.cloned.1.call-done = f32[24,2304]{1,0:T(8,128)} async-done(((f32[768,2304]{1,0:T(8,128)}), f32[24,2304]{1,0:T(8,128)}) %reduce-scatter.18.cloned.1.call-update) | async-done | bytes 221200 | tf_op jit(solution)/shard_map/reduce_scatter | solution.py:248
  (330 shorter events, 163.1 us)
Async XLA Ops:
  7.2 355.8 %copy-start = (bf16[768,16]{0,1:T(8,128)(2,1)S(1)}, bf16[768,16]{0,1:T(8,128)(2,1)}, u32[]{:S(2)}) copy-start(bf16[768,16]{0,1:T(8,128)(2,1)} %param.21) | copy-start | bytes 73732
  7.2 77.6 %all-gather.11.cloned.1.call-start = ((), (), s32[]{:S(2)}) async-start(), calls=%async_computation.16 | async-start | bytes 3760128 | tf_op jit(solution)/shard_map/all_gather | solution.py:68
  7.9 103.1 %all-gather.21.cloned.1.call-start = ((), (), s32[]{:S(2)}) async-start(), calls=%async_computation.21 | async-start | bytes 2359296 | tf_op jit(solution)/shard_map/all_gather | solution.py:102
  8.7 84.2 %copy-start.50 = (f32[768]{0:T(1024)}, f32[768]{0:T(1024)S(1)}, u32[]{:S(2)}) copy-start(f32[768]{0:T(1024)S(1)} %convert_element_type.215) | copy-start | bytes 9220
  10.3 74.5 %copy-start.59 = (f32[512]{0:T(512)}, f32[512]{0:T(512)S(1)}, u32[]{:S(2)}) copy-start(f32[512]{0:T(512)S(1)} %get-tuple-element.107) | copy-start | bytes 6148
  10.3 82.5 %copy-start.63 = (f32[512]{0:T(512)}, f32[512]{0:T(512)S(1)}, u32[]{:S(2)}) copy-start(f32[512]{0:T(512)S(1)} %get-tuple-element.108) | copy-start | bytes 6148
  11.0 73.8 %copy-start.67 = (f32[512]{0:T(512)}, f32[512]{0:T(512)S(1)}, u32[]{:S(2)}) copy-start(f32[512]{0:T(512)S(1)} %get-tuple-element.51) | copy-start | bytes 6148
  11.0 81.9 %copy-start.65 = (f32[512]{0:T(512)}, f32[512]{0:T(512)S(1)}, u32[]{:S(2)}) copy-start(f32[512]{0:T(512)S(1)} %get-tuple-element.50) | copy-start | bytes 6148
  11.0 73.8 %copy-start.61 = (f32[512]{0:T(512)}, f32[512]{0:T(512)S(1)}, u32[]{:S(2)}) copy-start(f32[512]{0:T(512)S(1)} %fusion.160) | copy-start | bytes 6148
  90.3 47.1 %all-gather.19.cloned.1.call-start = ((), (), s32[]{:S(2)}) async-start(), calls=%async_computation.20 | async-start | bytes 2359296 | tf_op jit(solution)/shard_map/all_gather | solution.py:103
  91.0 80.9 %all-gather.17.cloned.1.call-start = ((), (), s32[]{:S(2)}) async-start(), calls=%async_computation.19 | async-start | bytes 1253376 | tf_op jit(solution)/shard_map/all_gather | solution.py:69
  91.6 91.0 %all-gather.15.cloned.1.call-start = ((), (), s32[]{:S(2)}) async-start(), calls=%async_computation.18 | async-start | bytes 2359296 | tf_op jit(solution)/shard_map/all_gather | solution.py:102
  91.7 14.6 %copy-start.54 = (s32[1,1,512,1]{2,3,1,0:T(1,128)}, s32[1,1,512,1]{2,3,1,0:T(1,128)S(1)}, u32[]{:S(2)}) copy-start(s32[1,1,512,1]{2,3,1,0:T(1,128)S(1)} %get-tuple-element.79) | copy-start | bytes 6148
  91.7 443.2 %copy-start.57 = (s32[1,1,512,1]{2,3,1,0:T(1,128)}, s32[1,1,512,1]{2,3,1,0:T(1,128)S(1)}, u32[]{:S(2)}) copy-start(s32[1,1,512,1]{2,3,1,0:T(1,128)S(1)} %get-tuple-element.78) | copy-start | bytes 6148
  98.4 113.9 %all-gather.13.cloned.1.call-start = ((), (), s32[]{:S(2)}) async-start(), calls=%async_computation.17 | async-start | bytes 2359296 | tf_op jit(solution)/shard_map/all_gather | solution.py:103
  125.5 14.5 %copy-start.48 = (f32[12,512]{1,0:T(8,128)}, f32[12,512]{1,0:T(8,128)S(1)}, u32[]{:S(2)}) copy-start(f32[12,512]{1,0:T(8,128)S(1)} %get-tuple-element.96) | copy-start | bytes 73732
  137.3 15.4 %copy-start.52 = (f32[12,512]{1,0:T(8,128)}, f32[12,512]{1,0:T(8,128)S(1)}, u32[]{:S(2)}) copy-start(f32[12,512]{1,0:T(8,128)S(1)} %fusion.1) | copy-start | bytes 73732
  185.6 15.0 %copy-start.17 = (pred[512,1024]{1,0:T(8,128)(4,1)S(1)}, pred[512,1024]{1,0:T(8,128)(4,1)}, u32[]{:S(2)}) copy-start(pred[512,1024]{1,0:T(8,128)(4,1)} %get-tuple-element.90) | copy-start | bytes 1572868
  229.0 134.0 %copy-start.21 = (bf16[512,768]{1,0:T(8,128)(2,1)}, bf16[512,768]{1,0:T(8,128)(2,1)S(1)}, u32[]{:S(2)}) copy-start(bf16[512,768]{1,0:T(8,128)(2,1)S(1)} %get-tuple-element.81) | copy-start | bytes 2359300
  229.0 182.1 %copy-start.23 = (bf16[512,768]{1,0:T(8,128)(2,1)}, bf16[512,768]{1,0:T(8,128)(2,1)S(1)}, u32[]{:S(2)}) copy-start(bf16[512,768]{1,0:T(8,128)(2,1)S(1)} %get-tuple-element.80) | copy-start | bytes 2359300
  231.2 41.2 %all-to-all-start.2 = ((bf16[16,64,768]{2,1,0:T(8,128)(2,1)}), bf16[16,64,768]{2,1,0:T(8,128)(2,1)}, u32[]{:S(2)}, u32[]{:S(2)}) async-start(bf16[16,64,768]{2,1,0:T(8,128)(2,1)} %bitcast.313), calls=%async_computation.2 | async-start | bytes 3145728 | tf_op jit(solution)/shard_map/all_to_all | solution.py:143
  272.3 42.1 %all-to-all-start = ((bf16[16,64,768]{2,1,0:T(8,128)(2,1)}), bf16[16,64,768]{2,1,0:T(8,128)(2,1)}, u32[]{:S(2)}, u32[]{:S(2)}) async-start(bf16[16,64,768]{2,1,0:T(8,128)(2,1)} %bitcast.316), calls=%async_computation | async-start | bytes 3145728 | tf_op jit(solution)/shard_map/all_to_all | solution.py:143
  314.4 41.0 %all-to-all-start.3 = ((bf16[16,64,768]{2,1,0:T(8,128)(2,1)}), bf16[16,64,768]{2,1,0:T(8,128)(2,1)}, u32[]{:S(2)}, u32[]{:S(2)}) async-start(bf16[16,64,768]{2,1,0:T(8,128)(2,1)} %bitcast.317), calls=%async_computation.3 | async-start | bytes 3145728 | tf_op jit(solution)/shard_map/all_to_all | solution.py:150
  344.4 18.6 %copy-start.55 = (s32[1,1,512,1]{2,3,1,0:T(1,128)S(1)}, s32[1,1,512,1]{2,3,1,0:T(1,128)}, u32[]{:S(2)}) copy-start(s32[1,1,512,1]{2,3,1,0:T(1,128)} %copy-done.54) | copy-start | bytes 6148
  355.5 41.1 %all-to-all-start.1 = ((bf16[16,64,768]{2,1,0:T(8,128)(2,1)}), bf16[16,64,768]{2,1,0:T(8,128)(2,1)}, u32[]{:S(2)}, u32[]{:S(2)}) async-start(bf16[16,64,768]{2,1,0:T(8,128)(2,1)} %bitcast.315), calls=%async_computation.1 | async-start | bytes 3145728 | tf_op jit(solution)/shard_map/all_to_all | solution.py:150
  401.3 135.1 %copy-start.77 = (f32[512]{0:T(512)}, f32[512]{0:T(512)S(1)}, u32[]{:S(2)}) copy-start(f32[512]{0:T(512)S(1)} %get-tuple-element.88) | copy-start | bytes 6148
  403.7 40.9 %all-to-all-start.6 = ((bf16[16,64,768]{2,1,0:T(8,128)(2,1)}), bf16[16,64,768]{2,1,0:T(8,128)(2,1)}, u32[]{:S(2)}, u32[]{:S(2)}) async-start(bf16[16,64,768]{2,1,0:T(8,128)(2,1)} %bitcast.318), calls=%async_computation.8 | async-start | bytes 3145728 | tf_op jit(solution)/shard_map/all_to_all | solution.py:167
  411.4 156.6 %copy-start.79 = (f32[512]{0:T(512)}, f32[512]{0:T(512)S(1)}, u32[]{:S(2)}) copy-start(f32[512]{0:T(512)S(1)} %get-tuple-element.86) | copy-start | bytes 6148
  444.6 41.0 %all-to-all-start.4 = ((bf16[16,64,768]{2,1,0:T(8,128)(2,1)}), bf16[16,64,768]{2,1,0:T(8,128)(2,1)S(1)}, u32[]{:S(2)}, u32[]{:S(2)}) async-start(bf16[16,64,768]{2,1,0:T(8,128)(2,1)} %bitcast.319), calls=%async_computation.4 | async-start | bytes 3145728 | tf_op jit(solution)/shard_map/all_to_all | solution.py:167
  485.6 22.0 %copy-start.38 = (bf16[16,64,768]{2,1,0:T(8,128)(2,1)}, bf16[16,64,768]{2,1,0:T(8,128)(2,1)S(1)}, u32[]{:S(2)}) copy-start(bf16[16,64,768]{2,1,0:T(8,128)(2,1)S(1)} %all-to-all-done.4) | copy-start | bytes 4718596
  485.6 41.4 %all-to-all-start.7 = ((bf16[16,64,768]{2,1,0:T(8,128)(2,1)}), bf16[16,64,768]{2,1,0:T(8,128)(2,1)}, u32[]{:S(2)}, u32[]{:S(2)}) async-start(bf16[16,64,768]{2,1,0:T(8,128)(2,1)} %bitcast.320), calls=%async_computation.9 | async-start | bytes 3145728 | tf_op jit(solution)/shard_map/all_to_all | solution.py:183
  527.0 40.9 %all-to-all-start.5 = ((bf16[16,64,768]{2,1,0:T(8,128)(2,1)}), bf16[16,64,768]{2,1,0:T(8,128)(2,1)}, u32[]{:S(2)}, u32[]{:S(2)}) async-start(bf16[16,64,768]{2,1,0:T(8,128)(2,1)} %bitcast.314), calls=%async_computation.5 | async-start | bytes 3145728 | tf_op jit(solution)/shard_map/all_to_all | solution.py:183
  534.4 222.9 %reduce-scatter.10.cloned.1.call-start = ((), (), s32[]{:S(2)}) async-start(), calls=%async_computation.22 | async-start | bytes 2359296 | tf_op jit(solution)/shard_map/reduce_scatter | solution.py:225
  536.5 31.5 %copy-start.7 = (f32[512,768]{1,0:T(8,128)S(1)}, f32[512,768]{1,0:T(8,128)}, u32[]{:S(2)}) copy-start(f32[512,768]{1,0:T(8,128)} %copy-done.6) | copy-start | bytes 4718596
  600.3 16.9 %copy-start.20 = (bf16[512,768]{0,1:T(8,128)(2,1)S(1)}, bf16[512,768]{0,1:T(8,128)(2,1)}, u32[]{:S(2)}) copy-start(bf16[512,768]{0,1:T(8,128)(2,1)} %copy.56) | copy-start | bytes 2359300
  622.2 135.1 %reduce-scatter.12.cloned.1.call-start = ((), (), s32[]{:S(2)}) async-start(), calls=%async_computation.23 | async-start | bytes 2359296 | tf_op jit(solution)/shard_map/reduce_scatter | solution.py:231
  625.6 13.8 %copy-start.16 = (pred[512,1024]{1,0:T(8,128)(4,1)S(1)}, pred[512,1024]{1,0:T(8,128)(4,1)}, u32[]{:S(2)}) copy-start(pred[512,1024]{1,0:T(8,128)(4,1)} %get-tuple-element.91) | copy-start | bytes 1572868
  639.4 124.8 %reduce-scatter.14.cloned.1.call-start = ((), (), s32[]{:S(2)}) async-start(), calls=%async_computation.24 | async-start | bytes 2359296 | tf_op jit(solution)/shard_map/reduce_scatter | solution.py:225
  658.6 16.9 %copy-start.19 = (bf16[512,768]{0,1:T(8,128)(2,1)S(1)}, bf16[512,768]{0,1:T(8,128)(2,1)}, u32[]{:S(2)}) copy-start(bf16[512,768]{0,1:T(8,128)(2,1)} %copy.60) | copy-start | bytes 2359300
  680.5 83.6 %reduce-scatter.16.cloned.1.call-start = ((), (), s32[]{:S(2)}) async-start(), calls=%async_computation.25 | async-start | bytes 2359296 | tf_op jit(solution)/shard_map/reduce_scatter | solution.py:231
  694.3 145.3 %reduce-scatter.24.cloned.1.call-start = ((), (), s32[]{:S(2)}) async-start(), calls=%async_computation.29 | async-start | bytes 7077888 | tf_op jit(solution)/shard_map/reduce_scatter | solution.py:257
  714.1 136.0 %reduce-scatter.22.cloned.1.call-start = ((), (), s32[]{:S(2)}) async-start(), calls=%async_computation.28 | async-start | bytes 7077888 | tf_op jit(solution)/shard_map/reduce_scatter | solution.py:254
  731.8 122.9 %reduce-scatter.20.cloned.1.call-start = ((), (), s32[]{:S(2)}) async-start(), calls=%async_computation.27 | async-start | bytes 2433024 | tf_op jit(solution)/shard_map/reduce_scatter | solution.py:249
  736.1 242.2 %reduce-scatter.18.cloned.1.call-start = ((), (), s32[]{:S(2)}) async-start(), calls=%async_computation.26 | async-start | bytes 7299072 | tf_op jit(solution)/shard_map/reduce_scatter | solution.py:248
  785.0 49.0 %copy-start.12 = (f32[512,768]{1,0:T(8,128)S(1)}, f32[512,768]{1,0:T(8,128)}, u32[]{:S(2)}) copy-start(f32[512,768]{1,0:T(8,128)} %copy-done.11) | copy-start | bytes 4718596
  785.0 49.0 %copy-start.74 = (f32[512]{0:T(512)S(1)}, f32[512]{0:T(512)}, u32[]{:S(2)}) copy-start(f32[512]{0:T(512)} %copy-done.73) | copy-start | bytes 6148
  785.0 49.0 %copy-start.76 = (f32[512]{0:T(512)S(1)}, f32[512]{0:T(512)}, u32[]{:S(2)}) copy-start(f32[512]{0:T(512)} %copy-done.75) | copy-start | bytes 6148
  844.1 134.3 %copy-start.1 = (bf16[768,16]{0,1:T(8,128)(2,1)S(1)}, bf16[768,16]{0,1:T(8,128)(2,1)}, u32[]{:S(2)}) copy-start(bf16[768,16]{0,1:T(8,128)(2,1)} %param.21) | copy-start | bytes 73732
  (69 other events, 288.5 us)
Sparse Core Ops, SparseCore 0:
  10.8 73.9 all-gather.10
  90.4 8.3 all-gather.20
  100.9 10.9 all-gather.18
  114.6 57.3 all-gather.16
  173.9 8.6 all-gather.14
  184.6 10.9 all-gather.12
  622.3 10.7 reduce-scatter.9
  639.5 10.7 reduce-scatter.11
  680.7 11.1 reduce-scatter.13
  694.6 11.2 reduce-scatter.15
  714.3 14.8 reduce-scatter.23
  732.0 14.8 reduce-scatter.21
  752.8 100.2 reduce-scatter.19
  860.1 118.1 reduce-scatter.17
where the time goes:
time: 992 us; the launch traced here: 985 us
  waiting for transfers between devices  382 us (39%)
  matrix products  336 us (34%)
  other arithmetic  88.3 us (9%)
  starting transfers between devices  60.9 us (6%)
  blocking collectives  52.8 us (5%)
  local copies, waits for them, and re-layouts  50.1 us (5%)
  between operations  15.6 us (2%)
    reduce_scatter x1, waiting for transfers between devices, body(): lax.psum_scatter(grad_qkv_sum, ('ctx', 'shard'), scatter_dimension=0, til...  124 us
    all_gather x1, waiting for transfers between devices, body(): lax.all_gather(qkv_weight, 'shard', axis=0, tiled=True)  73.8 us
    dot_general x12, matrix products, rows_first(): lax.dot_general(left, right, (((0,), (0,)), ((), ())), preferred_element_...  73.6 us
    dot_general x8, matrix products, rows_last(): lax.dot_general(left, right, (((1,), (1,)), ((), ())), preferred_element_...  57.5 us
    unnamed x1, blocking collectives  45.5 us
    all_to_all x2, waiting for transfers between devices, body(): lax.all_to_all(outbound, 'shard', split_axis=0, concat_axis=0, tiled=True)  41.8 us
    all_to_all x2, waiting for transfers between devices, body(): lax.all_to_all(result.reshape(received.shape), 'shard', split_axis=0, con...  40.4 us
    all_to_all x2, waiting for transfers between devices, body(): lax.all_to_all(grad_outbound.reshape(experts, capacity, D), 'shard', spli...  36.7 us
  transfers between devices with their start and end apart: 22, of which 12 were waited for; matrix products, arithmetic and copies ran while one was open for 37% of the time, Pallas kernels for 0%

commit v1 on v0

--- a/solution.py
+++ b/solution.py
@@ -1,6 +1,10 @@
+import functools
+
 import jax
 import jax.numpy as jnp
 from jax import lax
+from jax.experimental import pallas as pl
+from jax.experimental.pallas import tpu as pltpu
 from jax.sharding import PartitionSpec as P
 
 D = 768
@@ -273,7 +277,877 @@
     )
 
 
+BF = jnp.bfloat16
+F32 = jnp.float32
+QB = 256
+GELU_K = 0.7978845608028654
+VMEM_WHOLE = pl.BlockSpec(memory_space=pltpu.VMEM)
+
+
+def nn(left, right):
+    return lax.dot_general(left, right, (((1,), (0,)), ((), ())), preferred_element_type=F32)
+
+
+def nt(left, right):
+    return lax.dot_general(left, right, (((1,), (1,)), ((), ())), preferred_element_type=F32)
+
+
+def tn(left, right):
+    return lax.dot_general(left, right, (((0,), (0,)), ((), ())), preferred_element_type=F32)
+
+
+def lanes_of(shape, half):
+    lane = lax.broadcasted_iota(jnp.int32, shape, 1)
+    return (lane < HEAD_DIM) if half == 0 else (lane >= HEAD_DIM)
+
+
+def attend_kernel(h_ref, w_ref, doc_col_ref, code_row_ref, qkv_ref, o_ref, lse_ref):
+    seq, width = h_ref.shape[0], o_ref.shape[1]
+    scale = HEAD_DIM ** (-0.5)
+
+    def project(block, carry):
+        rows = pl.ds(block * QB, QB)
+        qkv_ref[rows, :] = nn(h_ref[rows, :], w_ref[:, 0 : 3 * width]).astype(BF)
+        return carry
+
+    lax.fori_loop(0, seq // QB, project, 0)
+    for block in range(seq // QB):
+        low, kend = block * QB, (block + 1) * QB
+        rows = slice(low, kend)
+        qpos = lax.broadcasted_iota(jnp.int32, (QB, kend), 0) + low
+        kpos = lax.broadcasted_iota(jnp.int32, (QB, kend), 1)
+        same = doc_col_ref[rows, :] == code_row_ref[:, 0:kend]
+        allowed = (same & (kpos < qpos)) | (kpos == qpos)
+        bias = jnp.where(allowed, 0.0, NEGATIVE).astype(F32)
+        lane = lax.broadcasted_iota(jnp.int32, (QB, 128), 1)
+
+        def pair(index, stats):
+            at = pl.multiple_of(index * 128, 128)
+            q = qkv_ref[rows, pl.ds(at, 128)] * jnp.asarray(scale, BF)
+            k = qkv_ref[0:kend, pl.ds(width + at, 128)]
+            v = qkv_ref[0:kend, pl.ds(2 * width + at, 128)]
+            outs = []
+            for half in range(2):
+                qm = jnp.where(lanes_of(q.shape, half), q, jnp.zeros_like(q))
+                s = nt(qm, k) + bias
+                top = jnp.max(s, axis=1, keepdims=True)
+                e = jnp.exp(s - top)
+                total = jnp.sum(e, axis=1, keepdims=True)
+                outs.append(nn(e.astype(BF), v) * (1.0 / total))
+                stats = jnp.where(lane == 2 * index + half, top + jnp.log(total), stats)
+            o_ref[rows, pl.ds(at, 128)] = jnp.where(
+                lanes_of(outs[0].shape, 0), outs[0], outs[1]
+            ).astype(BF)
+            return stats
+
+        stats = lax.fori_loop(0, width // 128, pair, jnp.zeros((QB, 128), F32))
+        lse_ref[:, rows] = jnp.transpose(stats)[0 : lse_ref.shape[0], :]
+
+
+def attend(h_all, w_own, doc_col, code_row):
+    seq, width = h_all.shape[0], D // 2
+    flops = 2 * seq * D * 3 * width + 4 * seq * seq * width
+    return pl.pallas_call(
+        attend_kernel,
+        out_shape=(
+            jax.ShapeDtypeStruct((seq, 3 * width), BF),
+            jax.ShapeDtypeStruct((seq, width), BF),
+            jax.ShapeDtypeStruct((8, seq), F32),
+        ),
+        in_specs=[VMEM_WHOLE] * 4,
+        out_specs=(VMEM_WHOLE,) * 3,
+        compiler_params=pltpu.CompilerParams(vmem_limit_bytes=48 << 20),
+        cost_estimate=pl.CostEstimate(
+            flops=4 * flops, bytes_accessed=8 << 20, transcendentals=seq * seq * width // 128
+        ),
+        name="attend",
+    )(h_all, w_own, doc_col, code_row)
+
+
+def attend_back_kernel(has_prev, *refs):
+    if has_prev:
+        (h_ref, w_ref, qkv_ref, do_ref, lse_ref, doc_row_ref, code_col_ref, prev_ref,
+         gw_ref, dh_ref, dqkv_ref, dk_ref, dv_ref, kt_ref) = refs
+    else:
+        (h_ref, w_ref, qkv_ref, do_ref, lse_ref, doc_row_ref, code_col_ref,
+         gw_ref, dh_ref, dqkv_ref, dk_ref, dv_ref, kt_ref) = refs
+    seq, width = do_ref.shape
+    scale = HEAD_DIM ** (-0.5)
+    dk_ref[...] = jnp.zeros_like(dk_ref)
+    dv_ref[...] = jnp.zeros_like(dv_ref)
+    kt_ref[...] = jnp.transpose(qkv_ref[:, width : 2 * width])
+    for block in range(seq // QB):
+        low, kend = block * QB, (block + 1) * QB
+        rows = slice(low, kend)
+        qpos = lax.broadcasted_iota(jnp.int32, (kend, QB), 1) + low
+        kpos = lax.broadcasted_iota(jnp.int32, (kend, QB), 0)
+        same = doc_row_ref[:, rows] == code_col_ref[0:kend, :]
+        allowed = (same & (kpos < qpos)) | (kpos == qpos)
+        bias = jnp.where(allowed, 0.0, NEGATIVE).astype(F32)
+
+        def pair(index, carry):
+            at = pl.multiple_of(index * 128, 128)
+            q = qkv_ref[rows, pl.ds(at, 128)] * jnp.asarray(scale, BF)
+            k = qkv_ref[0:kend, pl.ds(width + at, 128)]
+            v = qkv_ref[0:kend, pl.ds(2 * width + at, 128)]
+            do = do_ref[rows, pl.ds(at, 128)]
+            dqt = jnp.zeros((128, QB), F32)
+            dv = dk = None
+            for half in range(2):
+                keep = lanes_of(q.shape, half)
+                qm = jnp.where(keep, q, jnp.zeros_like(q))
+                dom = jnp.where(keep, do, jnp.zeros_like(do))
+                p = jnp.exp(nt(k, qm) + bias - lse_ref[pl.ds(2 * index + half, 1), rows])
+                dp = nt(v, dom)
+                delta = jnp.sum(p * dp, axis=0, keepdims=True)
+                ds = (p * (dp - delta)).astype(BF)
+                dv_half = nn(p.astype(BF), dom)
+                dk_half = nn(ds, qm)
+                dv = dv_half if dv is None else dv + dv_half
+                dk = dk_half if dk is None else dk + dk_half
+                kt = kt_ref[pl.ds(pl.multiple_of(at + half * HEAD_DIM, HEAD_DIM), HEAD_DIM), 0:kend]
+                dqt = nn(kt, ds) if half == 0 else jnp.concatenate([dqt, nn(kt, ds)], axis=0)
+            dv_ref[0:kend, pl.ds(at, 128)] += dv
+            dk_ref[0:kend, pl.ds(at, 128)] += dk
+            dqkv_ref[rows, pl.ds(at, 128)] = (jnp.transpose(dqt) * scale).astype(BF)
+            return carry
+
+        lax.fori_loop(0, width // 128, pair, 0)
+    dqkv_ref[:, width : 2 * width] = dk_ref[...].astype(BF)
+    dqkv_ref[:, 2 * width :] = dv_ref[...].astype(BF)
+
+    def spread(block, carry):
+        rows = pl.ds(block * QB, QB)
+        dh_ref[rows, :] = nt(dqkv_ref[rows, :], w_ref[:, 0 : 3 * width])
+        return carry
+
+    lax.fori_loop(0, seq // QB, spread, 0)
+
+    def weigh(block, carry):
+        cols = pl.ds(pl.multiple_of(block * 128, 128), 128)
+        grad = tn(h_ref[...], dqkv_ref[:, cols])
+        if has_prev:
+            grad = grad + prev_ref[:, cols]
+        gw_ref[:, cols] = grad.astype(gw_ref.dtype)
+        return carry
+
+    lax.fori_loop(0, 3 * width // 128, weigh, 0)
+
+
+def attend_back(h_all, w_own, qkv, do_all, lse, doc_row, code_col, prev):
+    seq, width = do_all.shape
+    flops = 2 * seq * D * 3 * width * 2 + 10 * seq * seq * width
+    args = [h_all, w_own, qkv, do_all, lse, doc_row, code_col]
+    if prev is not None:
+        args.append(prev)
+    return pl.pallas_call(
+        functools.partial(attend_back_kernel, prev is not None),
+        out_shape=(
+            jax.ShapeDtypeStruct((D, 3 * width), F32),
+            jax.ShapeDtypeStruct((seq, D), F32),
+        ),
+        in_specs=[VMEM_WHOLE] * len(args),
+        out_specs=(VMEM_WHOLE,) * 2,
+        scratch_shapes=[
+            pltpu.VMEM((seq, 3 * width), BF),
+            pltpu.VMEM((seq, width), F32),
+            pltpu.VMEM((seq, width), F32),
+            pltpu.VMEM((width, seq), BF),
+        ],
+        compiler_params=pltpu.CompilerParams(vmem_limit_bytes=56 << 20),
+        cost_estimate=pl.CostEstimate(
+            flops=4 * flops, bytes_accessed=16 << 20, transcendentals=seq * seq * width // 128
+        ),
+        name="attend_back",
+    )(*args)
+
+
+FB = 512
+
+
+def expert_kernel(has_prev, side_ref, h_ref, g_ref, c_ref, up_ref, down_ref, *refs):
+    if has_prev:
+        (prev_up_ref, prev_down_ref, y_ref, dh_ref, gc_ref, gup_ref, gdown_ref,
+         dz_ref, gate_ref, z_ref, acc_ref, a_ref, du_ref) = refs
+    else:
+        (y_ref, dh_ref, gc_ref, gup_ref, gdown_ref,
+         dz_ref, gate_ref, z_ref, acc_ref, a_ref, du_ref) = refs
+    step, steps = pl.program_id(0), pl.num_programs(0)
+    rows_all = h_ref.shape[0]
+    blocks = rows_all // QB
+
+    @pl.when(step == 0)
+    def _():
+        def start(block, carry):
+            rows = pl.ds(block * QB, QB)
+            logit = jnp.sum(h_ref[rows, :].astype(F32) * c_ref[...], axis=1, keepdims=True)
+            gate = 1.0 / (1.0 + jnp.exp(-logit))
+            gate_ref[rows, :] = gate
+            dz_ref[rows, :] = (gate * g_ref[rows, :].astype(F32)).astype(BF)
+            z_ref[rows, :] = jnp.zeros((QB, D), F32)
+            acc_ref[rows, :] = jnp.zeros((QB, D), F32)
+            return carry
+
+        lax.fori_loop(0, blocks, start, 0)
+
+    def forward(block, carry):
+        rows = pl.ds(block * QB, QB)
+        u = nn(h_ref[rows, :], up_ref[...])
+        square = u * u
+        t = jnp.tanh(GELU_K * u * (1.0 + 0.044715 * square))
+        a = (0.5 * u * (1.0 + t)).astype(BF)
+        slope = 0.5 * (1.0 + t) + 0.5 * u * (1.0 - t * t) * (
+            GELU_K * (1.0 + 3 * 0.044715 * square)
+        )
+        a_ref[rows, :] = a
+        z_ref[rows, :] += nn(a, down_ref[...])
+        du = (nt(dz_ref[rows, :], down_ref[...]) * slope).astype(BF)
+        du_ref[rows, :] = du
+        acc_ref[rows, :] += nt(du, up_ref[...])
+        return carry
+
+    lax.fori_loop(0, blocks, forward, 0)
+    gup = tn(h_ref[...], du_ref[...])
+    gdown = tn(a_ref[...], dz_ref[...])
+    if has_prev:
+        gup = gup + prev_up_ref[...]
+        gdown = gdown + prev_down_ref[...]
+    gup_ref[...] = gup
+    gdown_ref[...] = gdown
+
+    @pl.when(step == steps - 1)
+    def _():
+        def finish(block, total):
+            rows = pl.ds(block * QB, QB)
+            z = z_ref[rows, :].astype(BF).astype(F32)
+            gate = gate_ref[rows, :]
+            dgate = jnp.sum(g_ref[rows, :].astype(F32) * z, axis=1, keepdims=True)
+            dlogit = dgate * gate * (1.0 - gate)
+            y_ref[rows, :] = (gate * z).astype(BF)
+            dh_ref[rows, :] = (acc_ref[rows, :] + dlogit * c_ref[...]).astype(BF)
+            return total + jnp.sum(
+                dlogit * h_ref[rows, :].astype(F32), axis=0, keepdims=True
+            )
+
+        gc_ref[...] = lax.fori_loop(0, blocks, finish, jnp.zeros((1, D), F32))
+
+
+def expert(side, h_slots, g_slots, g_block, centre, up, down, prev):
+    rows = h_slots.shape[0]
+    ff = up.shape[1]
+    steps = ff // FB
+    half = steps // 2
+    whole = lambda step, side: (0, 0)
+    turn = lambda step, side: (step + half * (1 - side[0])) % steps
+    up_map = lambda step, side: (0, turn(step, side))
+    down_map = lambda step, side: (turn(step, side), 0)
+    in_specs = [
+        pl.BlockSpec((rows, D), whole, pipeline_mode=pl.Buffered(1)),
+        pl.BlockSpec((rows, D), lambda step, side: (g_block, 0), pipeline_mode=pl.Buffered(1)),
+        pl.BlockSpec((1, D), whole),
+        pl.BlockSpec((D, FB), up_map),
+        pl.BlockSpec((FB, D), down_map),
+    ]
+    up_at = lambda step, side: (0, step)
+    down_at = lambda step, side: (step, 0)
+    args = [h_slots, g_slots, centre, up, down]
+    if prev is not None:
+        in_specs += [pl.BlockSpec((D, FB), up_at), pl.BlockSpec((FB, D), down_at)]
+        args += list(prev)
+    flops = 12 * rows * D * ff
+    return pl.pallas_call(
+        functools.partial(expert_kernel, prev is not None),
+        out_shape=(
+            jax.ShapeDtypeStruct((rows, D), BF),
+            jax.ShapeDtypeStruct((rows, D), BF),
+            jax.ShapeDtypeStruct((1, D), F32),
+            jax.ShapeDtypeStruct((D, ff), F32),
+            jax.ShapeDtypeStruct((ff, D), F32),
+        ),
+        grid_spec=pltpu.PrefetchScalarGridSpec(
+            num_scalar_prefetch=1,
+            grid=(steps,),
+            in_specs=in_specs,
+            out_specs=(
+                pl.BlockSpec((rows, D), whole),
+                pl.BlockSpec((rows, D), whole),
+                pl.BlockSpec((1, D), whole),
+                pl.BlockSpec((D, FB), up_at),
+                pl.BlockSpec((FB, D), down_at),
+            ),
+            scratch_shapes=[
+                pltpu.VMEM((rows, D), BF),
+                pltpu.VMEM((rows, 1), F32),
+                pltpu.VMEM((rows, D), F32),
+                pltpu.VMEM((rows, D), F32),
+                pltpu.VMEM((rows, FB), BF),
+                pltpu.VMEM((rows, FB), BF),
+            ],
+        ),
+        compiler_params=pltpu.CompilerParams(vmem_limit_bytes=56 << 20),
+        cost_estimate=pl.CostEstimate(
+            flops=flops, bytes_accessed=40 << 20, transcendentals=rows * ff
+        ),
+        name="expert",
+    )(side, *args)
+
+
+def swap(array):
+    return lax.ppermute(array, "ctx", [(0, 1), (1, 0)])
+
+
+def half_of(array, index, axis):
+    size = array.shape[axis] // 2
+    return lax.dynamic_slice_in_dim(array, index * size, size, axis)
+
+
+def greet(peers):
+    barrier = pltpu.get_barrier_semaphore()
+    for peer in peers:
+        pl.semaphore_signal(
+            barrier, inc=1, device_id=peer, device_id_type=pl.DeviceIdType.MESH
+        )
+    pl.semaphore_wait(barrier, len(peers))
+
+
+def send(src, dst, send_sem, recv_sem, peer):
+    return pltpu.make_async_remote_copy(
+        src_ref=src,
+        dst_ref=dst,
+        send_sem=send_sem,
+        recv_sem=recv_sem,
+        device_id=peer,
+        device_id_type=pl.DeviceIdType.MESH,
+    )
+
+
+def places():
+    me, core = lax.axis_index("shard"), lax.axis_index("ctx")
+    z, y, x = me // 4, (me // 2) % 2, me % 2
+    along_y, along_x = me + 2 - 4 * y, me + 1 - 2 * x
+    first = along_y * (1 - core) + along_x * core
+    second = along_x * (1 - core) + along_y * core
+    far = 4 * z + 3 - me % 4
+    line = [z, z + 1 - 2 * (z % 2), (z + 2) % 4, 3 - z]
+    return me, first, second, far, line
+
+
+def gather_kernel(w_ref, out_ref, send_sem, recv_sem):
+    size = w_ref.shape[0]
+    me, first, second, far, line = places()
+    lines = [4 * z for z in line]
+
+    def rows(block):
+        return out_ref.at[pl.ds(pl.multiple_of(block * size, 16), size), :]
+
+    peers = [{"shard": lines[j] + me % 4} for j in (1, 2, 3)]
+    one, two = {"shard": first}, {"shard": second}
+    greet(peers + [one, two])
+    copies = []
+
+    def push(block, role, peer, src=None):
+        copy = send(
+            rows(block) if src is None else src,
+            rows(block),
+            send_sem.at[len(copies)],
+            recv_sem.at[role],
+            peer,
+        )
+        copy.start()
+        copies.append(copy)
+
+    def arrive(block, role):
+        send(rows(block), rows(block), send_sem.at[0], recv_sem.at[role], one).wait_recv()
+
+    push(me, 3, one, w_ref)
+    push(me, 7, two, w_ref)
+    for j in (1, 2, 3):
+        push(me, j - 1, peers[j - 1], w_ref)
+    out_ref[pl.ds(pl.multiple_of(me * size, 16), size), :] = w_ref[...]
+    arrive(lines[0] + first % 4, 3)
+    push(lines[0] + first % 4, 11, two)
+    for j in (1, 2, 3):
+        block = lines[j] + me % 4
+        arrive(block, j - 1)
+        push(block, 3 + j, one)
+        push(block, 7 + j, two)
+        if j > 1:
+            block = lines[j - 1] + first % 4
+            arrive(block, 3 + j - 1)
+            push(block, 11 + j - 1, two)
+    block = lines[3] + first % 4
+    arrive(block, 6)
+    push(block, 14, two)
+    for j in range(4):
+        arrive(lines[j] + second % 4, 7 + j)
+        arrive(lines[j] + far % 4, 11 + j)
+    for copy in copies:
+        copy.wait_send()
+
+
+def gather_weights(w_mine):
+    size, columns = w_mine.shape
+    return pl.pallas_call(
+        gather_kernel,
+        out_shape=jax.ShapeDtypeStruct((16 * size, columns), BF),
+        in_specs=[VMEM_WHOLE],
+        out_specs=VMEM_WHOLE,
+        scratch_shapes=[pltpu.SemaphoreType.DMA((15,)), pltpu.SemaphoreType.DMA((15,))],
+        compiler_params=pltpu.CompilerParams(
+            collective_id=0, has_side_effects=True, vmem_limit_bytes=16 << 20
+        ),
+        name="gather_weights",
+    )(w_mine)
+
+
+def scatter_kernel(
+    gw_ref, go_ref, rows_ref, total_ref, theirs_ref,
+    packed_ref, rx1_ref, rx2_ref, rx3_ref, tx1_ref, tx2_ref, sum_ref, small_ref,
+    send_sem, recv_sem,
+):
+    me, first, second, far, line = places()
+    core = lax.axis_index("ctx")
+    lines = [4 * z for z in line]
+    part = sum_ref.shape[0] // 2
+    wide, half = gw_ref.shape[1], go_ref.shape[1]
+    peers = [{"shard": lines[j] + me % 4} for j in (1, 2, 3)]
+    one, two, twin = {"shard": first}, {"shard": second}, {"ctx": 1 - core}
+    greet(peers + [one, two, twin])
+    small_ref[...] = jnp.transpose(rows_ref[...])
+
+    def pack(chunk, carry):
+        top = pl.ds(pl.multiple_of(chunk * part, 8), part)
+        low = pl.ds(pl.multiple_of(D // 2 + chunk * part, 8), part)
+        for ref, at, size in ((gw_ref, 0, wide), (go_ref, wide, half), (small_ref, wide + half, 128)):
+            both = jnp.concatenate([ref[top, :], ref[low, :]], axis=0)
+            packed_ref[chunk, :, at : at + size] = both.astype(BF)
+        return carry
+
+    lax.fori_loop(0, 16, pack, 0)
+    copies = []
+
+    def push(src, dst, role, peer):
+        copy = send(src, dst, send_sem.at[role], recv_sem.at[role], peer)
+        copy.start()
+        copies.append(copy)
+
+    def arrive(dst, role):
+        send(dst, dst, send_sem.at[role], recv_sem.at[role], one).wait_recv()
+
+    order = (3, 2, 1, 0)
+    for j in order:
+        push(packed_ref.at[lines[j] + far % 4], rx1_ref.at[j], j, two)
+    for j in order:
+        push(packed_ref.at[lines[j] + second % 4], rx1_ref.at[4 + j], 4 + j, two)
+    for j in order:
+        arrive(rx1_ref.at[j], j)
+        total = packed_ref[lines[j] + first % 4].astype(F32) + rx1_ref[j].astype(F32)
+        tx1_ref[j] = total.astype(BF)
+        push(tx1_ref.at[j], rx2_ref.at[j], 8 + j, one)
+    own = None
+    for j in order:
+        arrive(rx1_ref.at[4 + j], 4 + j)
+        total = packed_ref[lines[j] + me % 4].astype(F32) + rx1_ref[4 + j].astype(F32)
+        arrive(rx2_ref.at[j], 8 + j)
+        total = total + rx2_ref[j].astype(F32)
+        if j:
+            tx2_ref[j - 1] = total.astype(BF)
+            push(tx2_ref.at[j - 1], rx3_ref.at[j - 1], 11 + j, peers[j - 1])
+        else:
+            own = total
+    for j in (1, 2, 3):
+        arrive(rx3_ref.at[j - 1], 11 + j)
+        own = own + rx3_ref[j - 1].astype(F32)
+    sum_ref[...] = own
+    push(
+        sum_ref.at[pl.ds(pl.multiple_of((1 - core) * part, 8), part), :], theirs_ref, 15, twin
+    )
+    total_ref[...] = sum_ref[pl.ds(pl.multiple_of(core * part, 8), part), :]
+    arrive(theirs_ref, 15)
+    for copy in copies:
+        copy.wait_send()
+
+
+def scatter_grads(grad_w, grad_out, rows):
+    columns = grad_w.shape[1] + grad_out.shape[1] + 128
+    part = D // 32
+    chunk = (2 * part, columns)
+    return pl.pallas_call(
+        scatter_kernel,
+        out_shape=(
+            jax.ShapeDtypeStruct((part, columns), F32),
+            jax.ShapeDtypeStruct((part, columns), F32),
+        ),
+        in_specs=[VMEM_WHOLE] * 3,
+        out_specs=(VMEM_WHOLE,) * 2,
+        scratch_shapes=[
+            pltpu.VMEM((16,) + chunk, BF),
+            pltpu.VMEM((8,) + chunk, BF),
+            pltpu.VMEM((4,) + chunk, BF),
+            pltpu.VMEM((3,) + chunk, BF),
+            pltpu.VMEM((4,) + chunk, BF),
+            pltpu.VMEM((3,) + chunk, BF),
+            pltpu.VMEM(chunk, F32),
+            pltpu.VMEM((D, 128), F32),
+            pltpu.SemaphoreType.DMA((16,)),
+            pltpu.SemaphoreType.DMA((16,)),
+        ],
+        compiler_params=pltpu.CompilerParams(
+            collective_id=1, has_side_effects=True, vmem_limit_bytes=40 << 20
+        ),
+        name="scatter_grads",
+    )(grad_w, grad_out, rows)
+
+
+def normal(values):
+    centre = values - jnp.mean(values, axis=1, keepdims=True)
+    spread = jnp.mean(centre * centre, axis=1, keepdims=True)
+    scale = lax.rsqrt(spread + EPSILON)
+    return centre * scale, scale
+
+
+def normal_back(unit, scale, gain, grad):
+    pull = grad * gain
+    return scale * (
+        pull
+        - jnp.mean(pull, axis=1, keepdims=True)
+        - unit * jnp.mean(pull * unit, axis=1, keepdims=True)
+    )
+
+
+RB = 128
+
+
+def post_kernel(
+    x_ref, o_ref, wo_ref, gain_ref, target_ref, slots_ref, x1_ref, full_ref, h_ref, send_sem, recv_sem
+):
+    core = lax.axis_index("ctx")
+    rows, width = x_ref.shape[0], o_ref.shape[1]
+    twin = {"ctx": 1 - core}
+    mine = pl.ds(pl.multiple_of(core * width, 128), width)
+    greet([twin])
+    copy = send(
+        o_ref.at[pl.ds(pl.multiple_of((1 - core) * rows, 128), rows), :],
+        full_ref.at[:, mine],
+        send_sem,
+        recv_sem,
+        twin,
+    )
+    copy.start()
+    full_ref[:, mine] = o_ref[pl.ds(pl.multiple_of(core * rows, 128), rows), :]
+    copy.wait()
+
+    def norm(block, carry):
+        at = pl.ds(pl.multiple_of(block * RB, RB), RB)
+        value = x_ref[at, :].astype(F32) + nn(full_ref[at, :], wo_ref[...])
+        x1_ref[at, :] = value
+        h_ref[at, :] = (normal(value)[0] * gain_ref[...]).astype(BF)
+        return carry
+
+    lax.fori_loop(0, rows // RB, norm, 0)
+
+    def place(block, carry):
+        at = pl.multiple_of(block * QB, QB)
+        slot = lax.broadcasted_iota(jnp.int32, (QB, rows), 0) + at
+        pick = (slot == target_ref[...]).astype(F32).astype(BF)
+        slots_ref[pl.ds(at, QB), :] = nn(pick, h_ref[...]).astype(BF)
+        return carry
+
+    lax.fori_loop(0, slots_ref.shape[0] // QB, place, 0)
+
+
+def post(x, o_own, wo, gain, target, slots):
+    rows = x.shape[0]
+    return pl.pallas_call(
+        post_kernel,
+        out_shape=(
+            jax.ShapeDtypeStruct((slots, D), BF),
+            jax.ShapeDtypeStruct((rows, D), F32),
+            jax.ShapeDtypeStruct((rows, D), BF),
+        ),
+        in_specs=[VMEM_WHOLE] * 5,
+        out_specs=(VMEM_WHOLE,) * 3,
+        scratch_shapes=[
+            pltpu.VMEM((rows, D), BF),
+            pltpu.SemaphoreType.DMA,
+            pltpu.SemaphoreType.DMA,
+        ],
+        compiler_params=pltpu.CompilerParams(
+            collective_id=2, has_side_effects=True, vmem_limit_bytes=32 << 20
+        ),
+        cost_estimate=pl.CostEstimate(
+            flops=8 * rows * D * (D + slots), bytes_accessed=8 << 20, transcendentals=0
+        ),
+        name="post",
+    )(x, o_own, wo, gain, target)
+
+
+def fore_kernel(
+    dh_ref, target_ref, g_ref, x1_ref, gain_ref, wo_ref, full_ref, prev_out_ref, prev_two_ref,
+    do_ref, dx_ref, gout_ref, gtwo_ref, dy_ref, all_ref, send_sem, recv_sem,
+):
+    core = lax.axis_index("ctx")
+    rows, width = g_ref.shape[0], do_ref.shape[1]
+    slots = dh_ref.shape[0]
+    twin = {"ctx": 1 - core}
+    greet([twin])
+
+    def norm(block, total):
+        at = pl.ds(pl.multiple_of(block * RB, RB), RB)
+        slot = lax.broadcasted_iota(jnp.int32, (RB, slots), 1)
+        pick = (slot == target_ref[at, :]).astype(F32).astype(BF)
+        grad = nn(pick, dh_ref[...])
+        unit, scale = normal(x1_ref[at, :])
+        dx = g_ref[at, :].astype(F32) + normal_back(unit, scale, gain_ref[...], grad)
+        dx_ref[at, :] = dx
+        dy = dx.astype(BF)
+        dy_ref[at, :] = dy
+        all_ref[at, :] = nt(dy, wo_ref[...]).astype(BF)
+        return total + jnp.sum(grad * unit, axis=0, keepdims=True)
+
+    gtwo_ref[...] = prev_two_ref[...] + lax.fori_loop(
+        0, rows // RB, norm, jnp.zeros((1, D), F32)
+    )
+    mine = pl.ds(pl.multiple_of(core * rows, 128), rows)
+    copy = send(
+        all_ref.at[:, pl.ds(pl.multiple_of((1 - core) * width, 128), width)],
+        do_ref.at[mine, :],
+        send_sem,
+        recv_sem,
+        twin,
+    )
+    copy.start()
+    do_ref[mine, :] = all_ref[:, pl.ds(pl.multiple_of(core * width, 128), width)]
+    gout_ref[...] = prev_out_ref[...] + tn(full_ref[...], dy_ref[...])
+    copy.wait()
+
+
+def fore(dh, target, g, x1, gain, wo, full, prev_out, prev_two):
+    rows, slots = g.shape[0], dh.shape[0]
+    return pl.pallas_call(
+        fore_kernel,
+        out_shape=(
+            jax.ShapeDtypeStruct((2 * rows, D // 2), BF),
+            jax.ShapeDtypeStruct((rows, D), F32),
+            jax.ShapeDtypeStruct((D, D), F32),
+            jax.ShapeDtypeStruct((1, D), F32),
+        ),
+        in_specs=[VMEM_WHOLE] * 9,
+        out_specs=(VMEM_WHOLE,) * 4,
+        scratch_shapes=[
+            pltpu.VMEM((rows, D), BF),
+            pltpu.VMEM((rows, D), BF),
+            pltpu.SemaphoreType.DMA,
+            pltpu.SemaphoreType.DMA,
+        ],
+        compiler_params=pltpu.CompilerParams(
+            collective_id=3, has_side_effects=True, vmem_limit_bytes=40 << 20
+        ),
+        cost_estimate=pl.CostEstimate(
+            flops=8 * rows * D * (2 * D + slots), bytes_accessed=8 << 20, transcendentals=0
+        ),
+        name="fore",
+    )(dh, target, g, x1, gain, wo, full, prev_out, prev_two)
+
+
+def tail_kernel(
+    dh_ref, x_ref, dx_ref, gain_ref, prev_ref, grad_ref, gone_ref, tx_ref, rx_ref, send_sem, recv_sem
+):
+    core = lax.axis_index("ctx")
+    rows = x_ref.shape[0]
+    twin = {"ctx": 1 - core}
+    greet([twin])
+    tx_ref[...] = dh_ref[pl.ds(pl.multiple_of((1 - core) * rows, 128), rows), :].astype(BF)
+    copy = send(tx_ref, rx_ref, send_sem, recv_sem, twin)
+    copy.start()
+    copy.wait()
+
+    def norm(block, total):
+        off = pl.multiple_of(block * RB, RB)
+        at = pl.ds(off, RB)
+        grad = dh_ref[pl.ds(core * rows + off, RB), :] + rx_ref[at, :].astype(F32)
+        unit, scale = normal(x_ref[at, :].astype(F32))
+        grad_ref[at, :] = dx_ref[at, :] + normal_back(unit, scale, gain_ref[...], grad)
+        return total + jnp.sum(grad * unit, axis=0, keepdims=True)
+
+    gone_ref[...] = prev_ref[...] + lax.fori_loop(0, rows // RB, norm, jnp.zeros((1, D), F32))
+
+
+def tail(dh, x, dx, gain, prev):
+    rows = x.shape[0]
+    return pl.pallas_call(
+        tail_kernel,
+        out_shape=(
+            jax.ShapeDtypeStruct((rows, D), F32),
+            jax.ShapeDtypeStruct((1, D), F32),
+        ),
+        in_specs=[VMEM_WHOLE] * 5,
+        out_specs=(VMEM_WHOLE,) * 2,
+        scratch_shapes=[
+            pltpu.VMEM((rows, D), BF),
+            pltpu.VMEM((rows, D), BF),
+            pltpu.SemaphoreType.DMA,
+            pltpu.SemaphoreType.DMA,
+        ],
+        compiler_params=pltpu.CompilerParams(
+            collective_id=4, has_side_effects=True, vmem_limit_bytes=32 << 20
+        ),
+        cost_estimate=pl.CostEstimate(
+            flops=40 * rows * D, bytes_accessed=8 << 20, transcendentals=0
+        ),
+        name="tail",
+    )(dh, x, dx, gain, prev)
+
+
+def body_pair(
+    tokens,
+    cotangent,
+    segment_ids,
+    padding,
+    routes,
+    norm_one_gain,
+    qkv_weight,
+    out_weight,
+    norm_two_gain,
+    centroids,
+    expert_in,
+    expert_out,
+):
+    local_len = tokens.shape[2]
+    experts = centroids.shape[1]
+    capacity = max(2, 2 * local_len // experts)
+    slots = experts * capacity
+    width = D // 2
+    me = lax.axis_index("ctx")
+    other = 1 - me
+    gain_one = norm_one_gain.astype(F32)[None, :]
+    gain_two = norm_two_gain.astype(F32)[None, :]
+    slot_ids = jnp.arange(slots, dtype=jnp.int32)
+    expert_ids = jnp.arange(experts, dtype=jnp.int32)
+
+    rows_of = qkv_weight.shape[0]
+    w_mine = lax.dynamic_index_in_dim(
+        qkv_weight.reshape(rows_of, 3, 2, width), me, 2, keepdims=False
+    ).reshape(rows_of, 3 * width)
+    w_all = gather_weights(jnp.concatenate([w_mine, half_of(out_weight, me, 1)], axis=1))
+    out_full = lax.all_gather(w_all[:, 3 * width :], "ctx", axis=1, tiled=True)
+
+    targets = []
+    for micro in range(MICRO):
+        route = routes[micro, 0, :, 0]
+        choose = (route[:, None] == expert_ids[None, :]).astype(jnp.int32)
+        rank = jnp.sum(jnp.cumsum(choose, axis=0) * choose, axis=1) - 1
+        targets.append(route * capacity + rank)
+    g_out = jnp.concatenate(
+        [
+            jnp.dot(
+                (slot_ids[:, None] == targets[m][None, :]).astype(BF),
+                cotangent[m, 0],
+                preferred_element_type=F32,
+            )
+            .astype(BF)
+            .reshape(experts, capacity, D)
+            for m in range(MICRO)
+        ],
+        axis=1,
+    )
+    g_in = lax.all_to_all(g_out, "shard", split_axis=0, concat_axis=0, tiled=True)
+    g_in = g_in.reshape(-1, MICRO, capacity, D)
+    g_in = [g_in[:, m].reshape(-1, D) for m in range(MICRO)]
+
+    centre = lax.dynamic_slice_in_dim(centroids.astype(F32).T, lax.axis_index("shard"), 1, 0)
+    side = me.astype(jnp.int32).reshape(1)
+    shape = (experts, capacity, D)
+
+    kept = []
+    for m in range(MICRO):
+        normed = layer_norm(tokens[m, 0].astype(F32), gain_one)
+        h_all = lax.all_gather(normed.astype(BF), "ctx", axis=0, tiled=True)
+        doc_all = lax.all_gather(segment_ids[m, 0], "ctx", axis=0, tiled=True)
+        pad_all = lax.all_gather(padding[m, 0], "ctx", axis=0, tiled=True)
+        code = jnp.where(pad_all == 1, doc_all, -1)
+        qkv, o_own, lse = attend(h_all, w_all, doc_all[:, None], code[None, :])
+        outbound, x1, o_full = post(
+            tokens[m, 0], o_own, out_full, gain_two, targets[m][None, :], slots
+        )
+        received = lax.all_to_all(
+            outbound.reshape(shape), "shard", split_axis=0, concat_axis=0, tiled=True
+        )
+        kept.append((h_all, doc_all, code, qkv, o_full, lse, x1, received))
+
+    prev = None
+    back = []
+    grad_centre = jnp.zeros((1, D), F32)
+    for m in range(MICRO):
+        y, dh2, gc, gup, gdown = expert(
+            side, kept[m][-1].reshape(-1, D), g_in[m], 0, centre, expert_in[0], expert_out[0], prev
+        )
+        prev = (gup, gdown)
+        grad_centre = grad_centre + gc
+        dh2 = lax.all_to_all(dh2.reshape(shape), "shard", split_axis=0, concat_axis=0, tiled=True)
+        y = lax.all_to_all(y.reshape(shape), "shard", split_axis=0, concat_axis=0, tiled=True)
+        back.append((y.reshape(slots, D), dh2.reshape(slots, D)))
+    gup, gdown = prev
+    ff_half = gup.shape[1] // 2
+    grad_up = gup[:, ff_half:] + swap(gup[:, :ff_half].astype(BF)).astype(F32)
+    grad_down = gdown[ff_half:] + swap(gdown[:ff_half].astype(BF)).astype(F32)
+
+    block_list, input_list = [], []
+    grad_one = jnp.zeros((1, D), F32)
+    grad_two = jnp.zeros((1, D), F32)
+    grad_out = jnp.zeros((D, D), F32)
+    grad_w = None
+    for m in range(MICRO):
+        h_all, doc_all, code, qkv, o_full, lse, x1, _ = kept[m]
+        y, dh2 = back[m]
+        do_all, dx1, grad_out, grad_two = fore(
+            dh2, targets[m][:, None], cotangent[m, 0], x1, gain_two, out_full, o_full,
+            grad_out, grad_two,
+        )
+        grad_w, dh_part = attend_back(
+            h_all, w_all, qkv, do_all, lse, doc_all[None, :], code[:, None], grad_w
+        )
+        grad_in, grad_one = tail(dh_part, tokens[m, 0], dx1, gain_one, grad_one)
+        input_list.append(grad_in)
+        combine = (slot_ids[:, None] == targets[m][None, :]).astype(BF)
+        block_list.append((x1 + rows_first(combine, y)).astype(BF))
+
+    grad_out = half_of(grad_out, me, 1) + swap(half_of(grad_out, other, 1).astype(BF)).astype(F32)
+    column = (jnp.arange(128) == 2 + lax.axis_index("shard")).astype(F32)[:, None]
+    rows = jnp.concatenate(
+        [grad_one, grad_two, jnp.zeros((126, D), F32)], axis=0
+    ) + column * grad_centre
+    mine, theirs = scatter_grads(grad_w, grad_out, rows)
+    low = jnp.where(me == 0, mine, theirs)
+    high = jnp.where(me == 0, theirs, mine)
+    part = mine.shape[0]
+    grad_qkv = jnp.stack(
+        [
+            low[:, : 3 * width].reshape(part, 3, width),
+            high[:, : 3 * width].reshape(part, 3, width),
+        ],
+        axis=2,
+    ).reshape(part, 3 * D)
+    grad_out = jnp.concatenate(
+        [low[:, 3 * width : 4 * width], high[:, 3 * width : 4 * width]], axis=1
+    )
+    small = mine[:, 4 * width :] + theirs[:, 4 * width :]
+
+    return (
+        jnp.stack(block_list)[:, None],
+        jnp.stack(input_list)[:, None],
+        small[:, 0],
+        grad_qkv,
+        grad_out,
+        small[:, 1],
+        small[:, 2 : 2 + experts],
+        grad_up[None],
+        grad_down[None],
+    )
+
+
 def solution(mesh):
+    plan = body_pair if (mesh.shape["ctx"], mesh.shape["shard"]) == (2, 16) else body
     in_specs = (
         P(None, "shard", "ctx", None),
         P(None, "shard", "ctx", None),
@@ -299,4 +1173,4 @@
         P("shard", None, "ctx"),
         P("shard", "ctx", None),
     )
-    return jax.shard_map(body, mesh=mesh, in_specs=in_specs, out_specs=out_specs, check_vma=False)
+    return jax.shard_map(plan, mesh=mesh, in_specs=in_specs, out_specs=out_specs, check_vma=False)

time: 992 us -> 574 us (0.58)
  matrix products: 336 us -> 7.42 us
  waiting for transfers between devices: 382 us -> 63.8 us
  Pallas kernels: 0 us -> 300 us
  other arithmetic: 88.3 us -> 29.3 us
  starting transfers between devices: 60.9 us -> 47.5 us
    pallas_call x0 -> x14, Pallas kernels: none -> 300 us  [the longest x2 102 us: expert(): pl.pallas_call(functools.partial(expert_kernel, prev is not None), out_sh...]
    dot_general x38 -> x2, matrix products: 262 us -> 2.06 us  [body_pair(): jnp.dot((slot_ids[:, None] == targets[m][None, :]).astype(BF), cotangent[...]
    reduce_scatter x8 -> x0, waiting for transfers between devices: 124 us -> none  [the longest x1 124 us: body(): lax.psum_scatter(grad_qkv_sum, ('ctx', 'shard'), scatter_dimension=0, til...]
    all_to_all x8 -> x6, waiting for transfers between devices: 155 us -> 55.3 us  [the longest x2 30.3 us: body_pair(): lax.all_to_all(outbound.reshape(shape), 'shard', split_axis=0, concat_axi...]
    all_gather x6 -> x3, waiting for transfers between devices: 101 us -> 7.76 us  [the longest x2 7.76 us: body_pair(): h_all = lax.all_gather(normed.astype(BF), 'ctx', axis=0, tiled=True)]
    dot_general x12 -> x2, matrix products: 73.6 us -> 5.37 us  [rows_first(): lax.dot_general(left, right, (((0,), (0,)), ((), ())), preferred_element_...]
    unnamed x1 -> x0, blocking collectives: 45.5 us -> none
    all_to_all x0 -> x1, blocking collectives: none -> 43.3 us  [body_pair(): lax.all_to_all(y.reshape(shape), 'shard', split_axis=0, concat_axis=0, ti...]
  transfers between devices with their start and end apart: 22 -> 12, of which waited for: 12 -> 4; matrix products, arithmetic and copies ran while one was open for 37% -> 9% of each run, Pallas kernels for 0% -> 46%
where the time goes in v1:
time: 574 us; the launch traced here: 565 us
  Pallas kernels  300 us (52%)
  waiting for transfers between devices  63.8 us (11%)
  blocking collectives  50.9 us (9%)
  local copies, waits for them, and re-layouts  50.7 us (9%)
  starting transfers between devices  47.5 us (8%)
  other arithmetic  29.3 us (5%)
  between operations  15 us (3%)
  matrix products  7.42 us (1%)
    pallas_call x2, Pallas kernels, expert(): pl.pallas_call(functools.partial(expert_kernel, prev is not None), out_sh...  102 us
    pallas_call x2, Pallas kernels, attend_back(): pl.pallas_call(functools.partial(attend_back_kernel, prev is not None), o...  64.7 us
    all_to_all x1, blocking collectives, body_pair(): lax.all_to_all(y.reshape(shape), 'shard', split_axis=0, concat_axis=0, ti...  43.3 us
    pallas_call x1, Pallas kernels, scatter_grads(): pl.pallas_call(scatter_kernel, out_shape=(jax.ShapeDtypeStruct((part, col...  35.3 us
    pallas_call x2, Pallas kernels, attend(): pl.pallas_call(attend_kernel, out_shape=(jax.ShapeDtypeStruct((seq, 3 * w...  32.3 us
    pallas_call x1, Pallas kernels, gather_weights(): pl.pallas_call(gather_kernel, out_shape=jax.ShapeDtypeStruct((16 * size,...  31.1 us
    all_to_all x2, waiting for transfers between devices, body_pair(): lax.all_to_all(outbound.reshape(shape), 'shard', split_axis=0, concat_axi...  30.3 us
    unnamed x106, local copies, waits for them, and re-layouts  24.9 us
  transfers between devices with their start and end apart: 12, of which 4 were waited for; matrix products, arithmetic and copies ran while one was open for 9% of the time, Pallas kernels for 46%

profile of v1, /device:TPU:0, one launch (start us, length us, event | category | flops | bytes accessed | tf_op | source)
XLA Modules:
  0.0 564.8 jit_solution(5008582172224076130)
XLA Ops:
  7.3 1.4 convert_reduce_fusion.1
  9.4 1.8 fusion.13
  11.6 1.7 fusion.15
  14.2 31.1 %gather_weights.1.w_ref.refs_1_ = bf16[768,1536]{1,0:T(8,128)(2,1)S(1)} custom-call(bf16[48,1536]{1,0:T(8,128)(2,1)S(1)} %pad_maximum_fusion.2.w_ref), custom_call_target="tpu_custom_call" | custom-call | tf_op jit(solution)/shard_map/gather_weights/pallas_call | solution.py:690
  46.4 2.4 slice_bitcast_fusion.3
  48.8 1.8 all-gather
  50.6 1.8 all-gather.1
  57.2 16.1 %attend.2 = (bf16[1024,1152]{1,0:T(8,128)(2,1)S(1)}, bf16[1024,384]{1,0:T(8,128)(2,1)S(1)}, f32[8,1024]{1,0:T(8,128)S(1)}) custom-call(bf16[1024,768]{1,0:T(8,128)(2,1)S(1)} %copy-done.14, bf16[768,1536]{1,0:T(8,128)(2,1)} %copy-done.2, s32[1024,1]{1,0:T(8,128)S(1)} %copy.56.doc_col_ref, s32[1,1024]{1,0:T(1,128)S(1)} %get-tuple-element.140.code_row_ref), custom_call_target="tpu_custom_call" | custom-call | flops 13690208256 | bytes 8388608 | tf_op jit(solution)/shard_map/attend/pallas_call | solution.py:350
  73.3 1.4 copy-done.32
  76.1 6.6 %post.2 = (bf16[1024,768]{1,0:T(8,128)(2,1)}, f32[512,768]{1,0:T(8,128)S(1)}, bf16[512,768]{1,0:T(8,128)(2,1)S(1)}) custom-call(bf16[512,768]{1,0:T(8,128)(2,1)S(1)} %copy-done.6, bf16[1024,384]{1,0:T(8,128)(2,1)S(1)} %get-tuple-element.49.o_ref, bf16[768,768]{1,0:T(8,128)(2,1)S(1)} %copy-done.16, f32[1,768]{1,0:T(1,128)S(1)} %reshape.260.gain_ref, ...), custom_call_target="tpu_custom_call" | custom-call | flops 5637144576 | bytes 8388608 | tf_op jit(solution)/shard_map/post/pallas_call | solution.py:861
  84.7 4.5 all-to-all-start
  91.4 1.9 pad_maximum_fusion
  93.2 30.3 %all-to-all-done = bf16[16,64,768]{2,1,0:T(8,128)(2,1)} async-done(((bf16[16,64,768]{2,1,0:T(8,128)(2,1)}), bf16[16,64,768]{2,1,0:T(8,128)(2,1)}, u32[]{:S(2)}, u32[]{:S(2)}) %all-to-all-start) | async-done | bytes 1572896 | tf_op jit(solution)/shard_map/all_to_all | solution.py:1073
  123.6 8.5 %all-to-all-start.1 = ((bf16[16,128,768]{2,1,0:T(8,128)(2,1)}), bf16[16,128,768]{2,1,0:T(8,128)(2,1)}, u32[]{:S(2)}, u32[]{:S(2)}) async-start(bf16[16,128,768]{2,1,0:T(8,128)(2,1)} %pad_maximum_fusion), calls=%async_computation.1 | async-start | bytes 6291456 | tf_op jit(solution)/shard_map/all_to_all | solution.py:1054
  132.8 1.8 all-gather.2
  134.8 2.2 all-gather.3
  138.3 7.7 %all-gather.12.cloned.1.call-done.h_ref.refs_0_ = bf16[1024,768]{1,0:T(8,128)(2,1)} async-done(((bf16[512,768]{1,0:T(8,128)(2,1)}), bf16[1024,768]{1,0:T(8,128)(2,1)}) %all-gather.12.cloned.1.call-update) | async-done | bytes 1572880 | tf_op jit(solution)/shard_map/all_gather | solution.py:1065
  146.1 1.4 copy-done.15
  147.5 16.2 %attend.3 = (bf16[1024,1152]{1,0:T(8,128)(2,1)S(1)}, bf16[1024,384]{1,0:T(8,128)(2,1)S(1)}, f32[8,1024]{1,0:T(8,128)S(1)}) custom-call(bf16[1024,768]{1,0:T(8,128)(2,1)S(1)} %copy-done.15, bf16[768,1536]{1,0:T(8,128)(2,1)} %copy-done.2, s32[1024,1]{1,0:T(8,128)S(1)} %copy.59.doc_col_ref, s32[1,1024]{1,0:T(1,128)S(1)} %get-tuple-element.142.code_row_ref), custom_call_target="tpu_custom_call" | custom-call | flops 13690208256 | bytes 8388608 | tf_op jit(solution)/shard_map/attend/pallas_call | solution.py:350
  165.7 6.5 %post.3 = (bf16[1024,768]{1,0:T(8,128)(2,1)}, f32[512,768]{1,0:T(8,128)S(1)}, bf16[512,768]{1,0:T(8,128)(2,1)S(1)}) custom-call(bf16[512,768]{1,0:T(8,128)(2,1)S(1)} %get-tuple-element.136.x_ref, bf16[1024,384]{1,0:T(8,128)(2,1)S(1)} %get-tuple-element.53.o_ref, bf16[768,768]{1,0:T(8,128)(2,1)S(1)} %copy-done.17, f32[1,768]{1,0:T(1,128)S(1)} %reshape.260.gain_ref, ...), custom_call_target="tpu_custom_call" | custom-call | flops 5637144576 | bytes 8388608 | tf_op jit(solution)/shard_map/post/pallas_call | solution.py:861
  173.4 19.5 %all-to-all-done.1 = bf16[16,128,768]{2,1,0:T(8,128)(2,1)} async-done(((bf16[16,128,768]{2,1,0:T(8,128)(2,1)}), bf16[16,128,768]{2,1,0:T(8,128)(2,1)}, u32[]{:S(2)}, u32[]{:S(2)}) %all-to-all-start.1) | async-done | bytes 3145760 | tf_op jit(solution)/shard_map/all_to_all | solution.py:1054
  192.9 14.4 %all-to-all-start.3 = ((bf16[16,64,768]{2,1,0:T(8,128)(2,1)}), bf16[16,64,768]{2,1,0:T(8,128)(2,1)}, u32[]{:S(2)}, u32[]{:S(2)}) async-start(bf16[16,64,768]{2,1,0:T(8,128)(2,1)} %bitcast.31), calls=%async_computation.3 | async-start | bytes 3145728 | tf_op jit(solution)/shard_map/all_to_all | solution.py:1073
  207.2 3.9 fusion.33
  211.1 50.4 %expert.2 = (bf16[1024,768]{1,0:T(8,128)(2,1)}, bf16[1024,768]{1,0:T(8,128)(2,1)}, f32[1,768]{1,0:T(1,128)}, f32[768,3072]{1,0:T(8,128)}, f32[3072,768]{1,0:T(8,128)}) custom-call(s32[1]{0:T(128)} %bitcast.8.side_ref, bf16[1024,768]{1,0:T(8,128)(2,1)} %bitcast.10.h_ref, bf16[1024,768]{1,0:T(8,128)(2,1)} %bitcast.133, f32[1,768]{1,0:T(1,128)} %fusion.28.c_ref, ...), custom_call_target="tpu_custom_call" | custom-call | flops 28991029248 | bytes 41943040 | tf_op jit(solution)/shard_map/expert/pallas_call | solution.py:558
  261.5 43.3 %all_to_all.35 = bf16[16,64,768]{2,1,0:T(8,128)(2,1)} all-to-all(bf16[16,64,768]{2,1,0:T(8,128)(2,1)} %bitcast.131), channel_id=1, replica_groups=mesh['ctx'=2,'shard'=16] {'shard'}, dimensions={0} | all-to-all | bytes 3145728 | tf_op jit(solution)/shard_map/all_to_all | solution.py:1088
  304.8 4.1 all-to-all-start.5
  308.8 51.4 %expert.3 = (bf16[1024,768]{1,0:T(8,128)(2,1)}, bf16[1024,768]{1,0:T(8,128)(2,1)}, f32[1,768]{1,0:T(1,128)}, f32[768,3072]{1,0:T(8,128)}, f32[3072,768]{1,0:T(8,128)}) custom-call(s32[1]{0:T(128)} %bitcast.8.side_ref, bf16[1024,768]{1,0:T(8,128)(2,1)} %bitcast.32.h_ref, bf16[1024,768]{1,0:T(8,128)(2,1)} %bitcast.132, f32[1,768]{1,0:T(1,128)} %fusion.28.c_ref, ...), custom_call_target="tpu_custom_call" | custom-call | flops 28991029248 | bytes 41943040 | tf_op jit(solution)/shard_map/expert/pallas_call | solution.py:558
  360.2 4.0 slice.173
  364.2 4.0 slice.174
  368.7 2.7 slice_bitcast_fusion.2
  371.4 7.2 %all-to-all-start.6 = ((bf16[16,64,768]{2,1,0:T(8,128)(2,1)}), bf16[16,64,768]{2,1,0:T(8,128)(2,1)}, u32[]{:S(2)}, u32[]{:S(2)}) async-start(bf16[16,64,768]{2,1,0:T(8,128)(2,1)} %bitcast.128), calls=%async_computation.6 | async-start | bytes 3145728 | tf_op jit(solution)/shard_map/all_to_all | solution.py:1087
  381.9 5.7 %add_bitcast_fusion = f32[1,1536,768]{2,1,0:T(8,128)} fusion(bf16[1536,768]{1,0:T(8,128)(2,1)} %collective-permute-done.2, f32[3072,768]{1,0:T(8,128)} %get-tuple-element.88), kind=kLoop, calls=%fused_computation.2 | loop fusion | flops 2359296 | bytes 11796480 | tf_op jit(solution)/shard_map/broadcast_in_dim | solution.py:1145
  387.6 6.1 %add_bitcast_fusion.1 = f32[1,768,1536]{2,1,0:T(8,128)} fusion(bf16[768,1536]{1,0:T(8,128)(2,1)} %collective-permute-done.1, f32[768,3072]{1,0:T(8,128)} %get-tuple-element.87), kind=kLoop, calls=%fused_computation.3 | loop fusion | flops 2359296 | bytes 11796480 | tf_op jit(solution)/shard_map/broadcast_in_dim | solution.py:1144
  393.7 2.1 fusion.16
  397.4 6.6 %fore.2 = (bf16[1024,384]{1,0:T(8,128)(2,1)S(1)}, f32[512,768]{1,0:T(8,128)S(1)}, f32[768,768]{1,0:T(8,128)S(1)}, f32[1,768]{1,0:T(1,128)S(1)}) custom-call(bf16[1024,768]{1,0:T(8,128)(2,1)S(1)} %bitcast.124, s32[512,1]{1,0:T(8,128)S(1)} %copy-done.13, bf16[512,768]{1,0:T(8,128)(2,1)S(1)} %copy-done.12, f32[512,768]{1,0:T(8,128)S(1)} %copy-done.21, ...), custom_call_target="tpu_custom_call" | custom-call | flops 8053063680 | bytes 8388608 | tf_op jit(solution)/shard_map/fore/pallas_call | solution.py:927
  407.4 5.5 all-to-all-done.6
  412.9 8.1 %all-to-all-start.4 = ((bf16[16,64,768]{2,1,0:T(8,128)(2,1)}), bf16[16,64,768]{2,1,0:T(8,128)(2,1)}, u32[]{:S(2)}, u32[]{:S(2)}) async-start(bf16[16,64,768]{2,1,0:T(8,128)(2,1)} %bitcast.127), calls=%async_computation.4 | async-start | bytes 3145728 | tf_op jit(solution)/shard_map/all_to_all | solution.py:1088
  424.8 1.7 copy-done.25
  427.6 7.9 %fore.3 = (bf16[1024,384]{1,0:T(8,128)(2,1)S(1)}, f32[512,768]{1,0:T(8,128)S(1)}, f32[768,768]{1,0:T(8,128)S(1)}, f32[1,768]{1,0:T(1,128)S(1)}) custom-call(bf16[1024,768]{1,0:T(8,128)(2,1)} %bitcast.47.dh_ref, s32[512,1]{1,0:T(8,128)S(1)} %copy.62.target_ref, bf16[512,768]{1,0:T(8,128)(2,1)S(1)} %copy-done.11, f32[512,768]{1,0:T(8,128)S(1)} %copy-done.23, ...), custom_call_target="tpu_custom_call" | custom-call | flops 8053063680 | bytes 8388608 | tf_op jit(solution)/shard_map/fore/pallas_call | solution.py:927
  435.5 1.5 copy-done.9
  438.1 31.7 %attend_back.2 = (f32[768,1152]{1,0:T(8,128)}, f32[1024,768]{1,0:T(8,128)}) custom-call(bf16[1024,768]{1,0:T(8,128)(2,1)} %all-gather.8.cloned.1.call-done.h_ref.refs_0_, bf16[768,1536]{1,0:T(8,128)(2,1)} %copy-done.2, bf16[1024,1152]{1,0:T(8,128)(2,1)} %copy-done.32, bf16[1024,384]{1,0:T(8,128)(2,1)} %copy-done.30, f32[8,1024]{1,0:T(8,128)} %copy-done.34, ...), custom_call_target="tpu_custom_call" | custom-call | flops 30601641984 | bytes 16777216 | tf_op jit(solution)/shard_map/attend_back/pallas_call | solution.py:443
  469.7 33.0 %attend_back.3 = (f32[768,1152]{1,0:T(8,128)}, f32[1024,768]{1,0:T(8,128)}) custom-call(bf16[1024,768]{1,0:T(8,128)(2,1)} %all-gather.12.cloned.1.call-done.h_ref.refs_0_, bf16[768,1536]{1,0:T(8,128)(2,1)} %copy-done.2, bf16[1024,1152]{1,0:T(8,128)(2,1)} %copy-done.33, bf16[1024,384]{1,0:T(8,128)(2,1)} %copy-done.31, f32[8,1024]{1,0:T(8,128)} %copy-done.35, ...), custom_call_target="tpu_custom_call" | custom-call | flops 30601641984 | bytes 16777216 | tf_op jit(solution)/shard_map/attend_back/pallas_call | solution.py:443
  502.7 3.2 fusion.17
  506.0 3.9 tail.2
  509.9 3.8 tail.3
  515.1 2.0 maximum_bitcast_fusion
  517.6 1.5 convert_add_fusion.go_ref
  519.2 35.3 %scatter_grads.1 = (f32[24,1664]{1,0:T(8,128)S(1)}, f32[24,1664]{1,0:T(8,128)S(1)}) custom-call(f32[768,1152]{1,0:T(8,128)S(1)} %copy-done.3, f32[768,384]{1,0:T(8,128)S(1)} %convert_add_fusion.go_ref, f32[128,768]{1,0:T(8,128)S(1)} %maximum_add_fusion.rows_ref), custom_call_target="tpu_custom_call" | custom-call | tf_op jit(solution)/shard_map/scatter_grads/pallas_call | solution.py:775
  (184 shorter events, 38.5 us)
Async XLA Ops:
  7.2 7.0 %copy-start = (bf16[48,768]{1,0:T(8,128)(2,1)S(1)}, bf16[48,768]{1,0:T(8,128)(2,1)}, u32[]{:S(2)}) copy-start(bf16[48,768]{1,0:T(8,128)(2,1)} %param.19) | copy-start | bytes 221188
  7.2 4.0 copy-start.36
  7.2 48.6 %all-gather.8.cloned.1.call-start = ((), (), s32[]{:S(2)}) async-start(), calls=%async_computation.7 | async-start | bytes 2359296 | tf_op jit(solution)/shard_map/all_gather | solution.py:1065
  11.6 1.8 copy-start.40
  13.3 61.5 %all-gather.10.cloned.1.call-start = ((), (), s32[]{:S(2)}) async-start(), calls=%async_computation.8 | async-start | bytes 1769472 | tf_op jit(solution)/shard_map/all_gather | solution.py:1033
  45.3 3.4 copy-start.2
  46.4 2.4 copy-start.49
  46.4 2.4 copy-start.45
  46.4 4.2 copy-start.46
  46.4 6.0 %copy-start.43 = (s32[2,1,512,1]{2,3,1,0:T(1,128)S(1)}, s32[2,1,512,1]{2,3,1,0:T(1,128)}, u32[]{:S(2)}) copy-start(s32[2,1,512,1]{2,3,1,0:T(1,128)} %param.16) | copy-start | bytes 12292
  50.6 22.8 %copy-start.41 = (s32[1,1,1024]{2,1,0:T(1,128)}, s32[1,1,1024]{2,1,0:T(1,128)S(1)}, u32[]{:S(2)}) copy-start(s32[1,1,1024]{2,1,0:T(1,128)S(1)} %all-gather) | copy-start | bytes 12292
  53.9 36.4 %copy-start.50 = (s32[512]{0:T(512)}, s32[512]{0:T(512)S(1)}, u32[]{:S(2)}) copy-start(s32[512]{0:T(512)S(1)} %get-tuple-element.155) | copy-start | bytes 6148
  55.8 1.4 copy-start.14
  57.2 17.6 %copy-start.6 = (bf16[512,768]{1,0:T(8,128)(2,1)S(1)}, bf16[512,768]{1,0:T(8,128)(2,1)}, u32[]{:S(2)}) copy-start(bf16[512,768]{1,0:T(8,128)(2,1)} %get-tuple-element.135.x_ref) | copy-start | bytes 2359300
  73.3 1.4 copy-start.32
  74.8 7.9 %copy-start.34 = (f32[8,1024]{1,0:T(8,128)}, f32[8,1024]{1,0:T(8,128)S(1)}, u32[]{:S(2)}) copy-start(f32[8,1024]{1,0:T(8,128)S(1)} %get-tuple-element.63.refs_4_) | copy-start | bytes 98308
  84.7 4.5 copy-start.37
  84.7 38.8 %all-to-all-start = ((bf16[16,64,768]{2,1,0:T(8,128)(2,1)}), bf16[16,64,768]{2,1,0:T(8,128)(2,1)}, u32[]{:S(2)}, u32[]{:S(2)}) async-start(bf16[16,64,768]{2,1,0:T(8,128)(2,1)} %bitcast.9), calls=%async_computation | async-start | bytes 3145728 | tf_op jit(solution)/shard_map/all_to_all | solution.py:1073
  123.6 69.3 %all-to-all-start.1 = ((bf16[16,128,768]{2,1,0:T(8,128)(2,1)}), bf16[16,128,768]{2,1,0:T(8,128)(2,1)}, u32[]{:S(2)}, u32[]{:S(2)}) async-start(bf16[16,128,768]{2,1,0:T(8,128)(2,1)} %pad_maximum_fusion), calls=%async_computation.1 | async-start | bytes 6291456 | tf_op jit(solution)/shard_map/all_to_all | solution.py:1054
  132.0 14.0 %all-gather.12.cloned.1.call-start = ((), (), s32[]{:S(2)}) async-start(), calls=%async_computation.9 | async-start | bytes 2359296 | tf_op jit(solution)/shard_map/all_gather | solution.py:1065
  134.6 29.1 %copy-start.42 = (s32[1,1,1024]{2,1,0:T(1,128)}, s32[1,1,1024]{2,1,0:T(1,128)S(1)}, u32[]{:S(2)}) copy-start(s32[1,1,1024]{2,1,0:T(1,128)S(1)} %all-gather.2) | copy-start | bytes 12292
  147.5 18.2 %copy-start.17 = (bf16[768,768]{1,0:T(8,128)(2,1)S(1)}, bf16[768,768]{1,0:T(8,128)(2,1)}, u32[]{:S(2)}) copy-start(bf16[768,768]{1,0:T(8,128)(2,1)} %all-gather.10.cloned.1.call-done.wo_ref) | copy-start | bytes 3538948
  173.4 19.5 %copy-start.28 = (bf16[512,768]{1,0:T(8,128)(2,1)}, bf16[512,768]{1,0:T(8,128)(2,1)S(1)}, u32[]{:S(2)}) copy-start(bf16[512,768]{1,0:T(8,128)(2,1)S(1)} %get-tuple-element.69.full_ref) | copy-start | bytes 2359300
  192.9 68.6 %all-to-all-start.3 = ((bf16[16,64,768]{2,1,0:T(8,128)(2,1)}), bf16[16,64,768]{2,1,0:T(8,128)(2,1)}, u32[]{:S(2)}, u32[]{:S(2)}) async-start(bf16[16,64,768]{2,1,0:T(8,128)(2,1)} %bitcast.31), calls=%async_computation.3 | async-start | bytes 3145728 | tf_op jit(solution)/shard_map/all_to_all | solution.py:1073
  304.8 66.6 %all-to-all-start.5 = ((bf16[16,64,768]{2,1,0:T(8,128)(2,1)}), bf16[16,64,768]{2,1,0:T(8,128)(2,1)S(1)}, u32[]{:S(2)}, u32[]{:S(2)}) async-start(bf16[16,64,768]{2,1,0:T(8,128)(2,1)} %bitcast.130), calls=%async_computation.5 | async-start | bytes 3145728 | tf_op jit(solution)/shard_map/all_to_all | solution.py:1087
  364.2 17.6 %collective-permute-start.2 = (bf16[1536,768]{1,0:T(8,128)(2,1)}, bf16[1536,768]{1,0:T(8,128)(2,1)}, u32[]{:S(2)}, u32[]{:S(2)}) collective-permute-start(bf16[1536,768]{1,0:T(8,128)(2,1)} %slice.173), channel_id=1, source_target_pairs={{0,16},{16,0},{1,17},{17,1},{2,18},{18,2},{3,19},{19,3},{4,20},{20... | collective-permute-start | bytes 7077896 | tf_op jit(solution)/shard_map/ppermute | solution.py:596
  368.2 19.3 %collective-permute-start.1 = (bf16[768,1536]{1,0:T(8,128)(2,1)}, bf16[768,1536]{1,0:T(8,128)(2,1)}, u32[]{:S(2)}, u32[]{:S(2)}) collective-permute-start(bf16[768,1536]{1,0:T(8,128)(2,1)} %slice.174), channel_id=1, source_target_pairs={{0,16},{16,0},{1,17},{17,1},{2,18},{18,2},{3,19},{19,3},{4,20},{20... | collective-permute-start | bytes 7077896 | tf_op jit(solution)/shard_map/ppermute | solution.py:596
  371.4 7.2 %copy-start.44 = (bf16[768]{0:T(1024)(128)(2,1)S(1)}, bf16[768]{0:T(1024)(128)(2,1)}, u32[]{:S(2)}) copy-start(bf16[768]{0:T(1024)(128)(2,1)} %param.17) | copy-start | bytes 4612
  371.4 41.5 %all-to-all-start.6 = ((bf16[16,64,768]{2,1,0:T(8,128)(2,1)}), bf16[16,64,768]{2,1,0:T(8,128)(2,1)}, u32[]{:S(2)}, u32[]{:S(2)}) async-start(bf16[16,64,768]{2,1,0:T(8,128)(2,1)} %bitcast.128), calls=%async_computation.6 | async-start | bytes 3145728 | tf_op jit(solution)/shard_map/all_to_all | solution.py:1087
  378.6 3.2 copy-start.47
  378.6 3.2 copy-start.48
  387.6 6.1 %copy-start.21 = (f32[512,768]{1,0:T(8,128)S(1)}, f32[512,768]{1,0:T(8,128)}, u32[]{:S(2)}) copy-start(f32[512,768]{1,0:T(8,128)} %copy-done.20) | copy-start | bytes 4718596
  387.6 6.1 %copy-start.38 = (bf16[16,64,768]{2,1,0:T(8,128)(2,1)S(1)}, bf16[16,64,768]{2,1,0:T(8,128)(2,1)}, u32[]{:S(2)}) copy-start(bf16[16,64,768]{2,1,0:T(8,128)(2,1)} %all_to_all.35) | copy-start | bytes 4718596
  393.7 2.3 copy-start.27
  395.8 1.6 copy-start.18
  412.9 89.8 %all-to-all-start.4 = ((bf16[16,64,768]{2,1,0:T(8,128)(2,1)}), bf16[16,64,768]{2,1,0:T(8,128)(2,1)}, u32[]{:S(2)}, u32[]{:S(2)}) async-start(bf16[16,64,768]{2,1,0:T(8,128)(2,1)} %bitcast.127), calls=%async_computation.4 | async-start | bytes 3145728 | tf_op jit(solution)/shard_map/all_to_all | solution.py:1088
  424.8 1.7 copy-start.25
  435.5 1.5 copy-start.9
  435.5 2.4 copy-start.31
  437.9 79.3 %collective-permute-start = (bf16[768,384]{1,0:T(8,128)(2,1)}, bf16[768,384]{1,0:T(8,128)(2,1)}, u32[]{:S(2)}, u32[]{:S(2)}) collective-permute-start(bf16[768,384]{1,0:T(8,128)(2,1)} %dynamic-slice_convert_fusion), channel_id=1, source_target_pairs={{0,16},{16,0},{1,17},{17,1},{2,18},{18,2},{3,19},{19,3},{4,20},{20... | collective-permute-start | bytes 1769480 | tf_op jit(solution)/shard_map/ppermute | solution.py:596
  469.7 33.0 %copy-start.51 = (s32[512]{0:T(512)S(1)}, s32[512]{0:T(512)}, u32[]{:S(2)}) copy-start(s32[512]{0:T(512)} %copy-done.50) | copy-start | bytes 6148
  502.7 3.3 copy-start.4
  502.7 3.3 copy-start.8
  506.0 3.9 copy-start.5
  509.9 3.9 copy-start.39
  515.1 2.5 copy-start.10
  515.1 4.1 copy-start.3
  555.2 2.6 copy-start.1
  (16 other events, 18.6 us)
Sparse Core Ops, SparseCore 0:
  13.4 12.4 all-gather.7
  46.5 7.4 all-gather.9
  135.0 11.0 all-gather.11
